TPU v7x, 32 devices: a whole 2x2x4 slice. The times are simulated.
32 devices in a mesh: member: 4 (over z), band: 4 (over y, core), tensor: 2 (over x).
Axes of the slice: x: 2, y: 2, z: 4, core: 2. Of those that a mesh axis runs over, the one named last changes fastest.
Arguments:
- prior_grids: bfloat16 [4, 4, 32, 128, 192], P('member', None, 'band'), may hold values from -6 to 6
- w_qkv: bfloat16 [192, 3, 192], P(None, None, 'tensor'), may hold values from -0.4375 to 0.4375
- w_out: bfloat16 [192, 192], P('tensor'), may hold values from -0.4375 to 0.4375
- w_up: bfloat16 [192, 768], P(None, 'tensor'), may hold values from -0.4375 to 0.4375
- w_down: bfloat16 [768, 192], P('tensor'), may hold values from -0.21875 to 0.21875
- head_weight: bfloat16 [192, 160], replicated, may hold values from -0.4375 to 0.4375
- pos_bias: bfloat16 [6, 128, 128], P('tensor'), may hold values from -6 to 400
- zonal_offsets: int32 [4], P('member'), may hold values from 0 to 127
- obs_index: int32 [2, 32, 128, 16], P('tensor', 'band', 'member'), may hold values from 0 to 319
- obs_count: int32 [2, 32, 128], P('tensor', 'band', 'member'), may hold values from 8 to 16
- obs_value: float32 [2, 32, 128, 16], P('tensor', 'band', 'member'), may hold values from -6 to 6
- obs_weight: float32 [2, 32, 128, 16], P('tensor', 'band', 'member'), may hold values from 1 to 30
Outputs:
- analysis: float32 [4, 4, 32, 128, 160], P(None, 'tensor', 'band', 'member')
All inputs are finite; a program needn't handle non-finite values.
Results may differ from a plain program's by a relative error of at most 0.025.
Values may be sent and summed in bfloat16 or wider, within the bound.
No kernel may reach another device: no remote copies, remote signals or barrier semaphores. Data moves between devices by JAX's collectives and lax.ppermute only.
A program may use at most 64 MiB of HBM per device.

v0:
```python
import functools
import math

import jax
import jax.numpy as jnp
from jax import lax
from jax.experimental import pallas as pl
from jax.experimental.pallas import tpu as pltpu
from jax.sharding import PartitionSpec as P


WLON = 8
NEWTON = 8
LANES = 128
GROUP = 4
LOG2E = 1.4426950408889634
F32 = jnp.float32
BF16 = jnp.bfloat16


VMEM = pltpu.VMEM
PARAMS = pltpu.CompilerParams(vmem_limit_bytes=32 * 1024 * 1024)


def near(x):
    return pltpu.with_memory_space_constraint(x, pltpu.VMEM)


def nn(a, b):
    return lax.dot_general(a, b, (((1,), (0,)), ((), ())), preferred_element_type=F32)


def nt(a, b):
    return lax.dot_general(a, b, (((1,), (1,)), ((), ())), preferred_element_type=F32)


def tn(a, b):
    return lax.dot_general(a, b, (((0,), (0,)), ((), ())), preferred_element_type=F32)


def eye(n):
    return (
        lax.broadcasted_iota(jnp.int32, (n, n), 0) == lax.broadcasted_iota(jnp.int32, (n, n), 1)
    ).astype(BF16)


def to_dense(x):
    half = x.shape[0] // 2
    return jnp.concatenate(
        [x[:, :LANES], jnp.concatenate([x[:half, LANES:], x[half:, LANES:]], axis=1)], axis=0
    )


def from_dense(d):
    rows = d.shape[0] * 2 // 3
    half = rows // 2
    part = LANES // 2
    high = jnp.concatenate([d[rows:, :part], d[rows:, part:]], axis=0)
    del half
    return jnp.concatenate([d[:rows], high], axis=1)


def pack_kernel(qkv, w_out, w_up, w_down, bias, a_ref, b_ref):
    ident = eye(qkv.shape[2])
    dense = to_dense(jnp.concatenate([nt(ident, qkv[i]).astype(BF16) for i in range(3)], axis=0))
    n_a = dense.shape[0]
    a_ref[:n_a] = dense
    heads, wtok, _ = bias.shape
    for h in range(heads):
        a_ref[n_a + h * wtok : n_a + (h + 1) * wtok] = bias[h]
    o = to_dense(w_out[...])
    r0 = o.shape[0]
    b_ref[:r0] = o
    up = to_dense(nt(eye(w_up.shape[1]), w_up[...]).astype(BF16))
    r1 = r0 + up.shape[0]
    b_ref[r0:r1] = up
    feats, ff = w_down.shape
    for i in range(ff // LANES):
        b_ref[r1 + i * feats : r1 + (i + 1) * feats] = w_down[:, i * LANES : (i + 1) * LANES]


def pack(qkv, w_out, w_up, w_down, bias):
    _, feats, e_loc = qkv.shape
    heads, wtok, _ = bias.shape
    ff = w_up.shape[1]
    a_rows = 3 * e_loc * 3 // 2 + heads * wtok
    b_rows = e_loc * 3 // 2 + ff * 3 // 2 + feats * (ff // LANES)
    vm = pl.BlockSpec(memory_space=pltpu.VMEM)
    return pl.pallas_call(
        pack_kernel,
        out_shape=(VMEM((a_rows, LANES), BF16), VMEM((b_rows, LANES), BF16)),
        in_specs=[vm] * 5,
        out_specs=[vm] * 2,
        compiler_params=PARAMS,
        name="pack",
    )(qkv, w_out, w_up, w_down, bias)


def prologue_kernel(offs, prior, above, below, hw_t, obs_i, obs_n, obs_v, obs_w, *refs):
    n_refs, raw_refs, hw, perm, idx, val, wgt, own, xscr, sem = refs[:2], refs[2:4], *refs[4:]
    levs, n_rows, feats, cols = own.shape
    half = n_rows // 2
    windows = cols // WLON
    start = lax.axis_index("tensor") * levs
    copy = pltpu.make_async_copy(prior.at[pl.ds(start, levs)], own, sem)
    copy.start()
    off = offs[0]
    me = lax.axis_index("member")
    dests = lax.axis_size("member")
    hw[...] = nt(eye(feats), hw_t[...]).astype(BF16)

    slot = lax.broadcasted_iota(jnp.int32, obs_i.shape[1:], 0)
    for side in range(2):
        at = range(side * half, (side + 1) * half)
        idx[side] = jnp.concatenate([obs_i[r] for r in at], axis=1)
        val[side] = jnp.concatenate([obs_v[r] for r in at], axis=1)
        wgt[side] = jnp.concatenate(
            [jnp.where(slot < obs_n[r : r + 1], obs_w[r], 0.0) for r in at], axis=1
        )

    j = lax.broadcasted_iota(jnp.int32, (cols, cols), 0) + off
    j = jnp.where(j >= cols, j - cols, j)
    rollm = (j == lax.broadcasted_iota(jnp.int32, (cols, cols), 1)).astype(BF16)

    cw = cols // dests
    patches = half * cw
    lane = lax.broadcasted_iota(jnp.int32, (cols, LANES), 1)
    col = lax.broadcasted_iota(jnp.int32, (cols, LANES), 0) + off
    col = jnp.where(col >= cols, col - cols, col)
    dest = col // cw
    base = (dest ^ me) * patches + (col - dest * cw)
    for r in range(half):
        for b in range(dests * patches // LANES):
            hit = base + r * cw == lane + b * LANES
            perm[r * cols : (r + 1) * cols, b * LANES : (b + 1) * LANES] = hit.astype(BF16)

    def norm(x):
        x = x.astype(F32)
        c = x - jnp.sum(x, axis=0, keepdims=True) * (1.0 / feats)
        v = jnp.sum(c * c, axis=0, keepdims=True) * (1.0 / feats)
        return (c * lax.rsqrt(v + 1e-05)).astype(BF16)

    def by_window(first, second):
        f = first.reshape(windows, 1, WLON, feats)
        s = second.reshape(windows, 1, WLON, feats)
        return jnp.concatenate([f, s], axis=1).reshape(windows, 2 * WLON, feats).astype(BF16)

    copy.wait()
    for side in range(2):
        halo = (above, below)[side]

        def one_level(lev, carry, side=side, halo=halo):
            for r in range(0, half, 2):
                x0, x1 = own[lev, side * half + r], own[lev, side * half + r + 1]
                own_row = half + r if side == 0 else r
                at = pl.multiple_of(lev * (n_rows * WLON) + own_row * WLON, 2 * WLON)
                n_refs[side][:, pl.ds(at, 2 * WLON), :] = by_window(
                    nt(rollm, norm(x0)), nt(rollm, norm(x1))
                )
                at = pl.multiple_of(lev * (half * WLON) + r * WLON, 2 * WLON)
                xscr[:, pl.ds(at, 2 * WLON), :] = by_window(nt(rollm, x0), nt(rollm, x1))
                h0, h1 = halo[lev, r], halo[lev, r + 1]
                halo_row = r if side == 0 else half + r
                at = pl.multiple_of(lev * (n_rows * WLON) + halo_row * WLON, 2 * WLON)
                n_refs[side][:, pl.ds(at, 2 * WLON), :] = by_window(
                    nt(rollm, norm(h0)), nt(rollm, norm(h1))
                )
            return carry

        lax.fori_loop(0, levs, one_level, 0)
        qtok = levs * half * WLON
        ident = eye(feats)
        for w in range(0, windows, GROUP):
            x = xscr[w : w + GROUP].reshape(GROUP * qtok, feats)
            raw_refs[side][:, w * qtok : (w + GROUP) * qtok] = nt(ident, x).astype(BF16)


def prologue(offs, prior_t, above, below, hw_t, obs, levs, dests):
    slots = obs[0].shape[1]
    patches = prior_t.shape[1] // 2 * (prior_t.shape[3] // dests)
    _, n_rows, feats, cols = prior_t.shape
    half = n_rows // 2
    windows = cols // WLON
    width = hw_t.shape[0]
    n_shape = VMEM((windows, levs * n_rows * WLON, feats), BF16)
    raw_shape = VMEM((feats, levs * half * cols), BF16)
    vm = pl.BlockSpec(memory_space=pltpu.VMEM)
    return pl.pallas_call(
        prologue_kernel,
        out_shape=(
            n_shape,
            n_shape,
            raw_shape,
            raw_shape,
            VMEM((feats, width), BF16),
            VMEM((half * cols, half * cols), BF16),
            VMEM((2, slots, patches), jnp.int32),
            VMEM((2, slots, patches), F32),
            VMEM((2, slots, patches), F32),
        ),
        in_specs=[pl.BlockSpec(memory_space=pltpu.SMEM), pl.BlockSpec(memory_space=pl.ANY)]
        + [vm] * 7,
        out_specs=[vm] * 9,
        scratch_shapes=[
            pltpu.VMEM((levs, n_rows, feats, cols), BF16),
            pltpu.VMEM((windows, levs * half * WLON, feats), BF16),
            pltpu.SemaphoreType.DMA,
        ],
        compiler_params=PARAMS,
        name="prologue",
    )(offs, prior_t, near(above), near(below), hw_t, *obs)


def gelu(x):
    return 0.5 * x * (1.0 + lax.erf(x * math.sqrt(0.5)))


def forecast_kernel(*refs, side, parts, dests, e_loc, heads_loc, ff_loc, levs, n_rows):
    n_ref, raw, hw, perm = refs[:4]
    a_parts = refs[4 : 4 + parts]
    b_parts = refs[4 + parts : 4 + 2 * parts]
    refs = refs[4 + 2 * parts :]
    outs = refs[:dests]
    (wq, wk, wv, wot, wup, wdt, bias, fscr) = refs[dests:]
    windows, wtok, feats = n_ref.shape
    half = n_rows // 2
    cols = windows * WLON
    qtok = levs * half * WLON
    heads = heads_loc * parts
    head_dim = e_loc // heads_loc
    width = hw.shape[1]
    q_row = half - half * side
    band = lax.axis_index("band")
    if side == 0:
        is_open = band > 0
    else:
        is_open = band < lax.axis_size("band") - 1
    penalty = jnp.where(is_open, 0.0, -1000000000.0).astype(F32)

    n_a = 3 * e_loc * 3 // 2
    r0 = e_loc * 3 // 2
    r1 = r0 + ff_loc * 3 // 2
    for p in range(parts):
        qkv = from_dense(a_parts[p][:n_a])
        rows = slice(p * e_loc, (p + 1) * e_loc)
        wq[rows] = qkv[:e_loc]
        wk[rows] = qkv[e_loc : 2 * e_loc]
        wv[rows] = qkv[2 * e_loc :]
        wup[p * ff_loc : (p + 1) * ff_loc] = from_dense(b_parts[p][r0:r1])
        for i in range(ff_loc // LANES):
            lo = p * ff_loc + i * LANES
            wdt[:, lo : lo + LANES] = b_parts[p][r1 + i * feats : r1 + (i + 1) * feats]
    w_out = jnp.concatenate([from_dense(b_parts[p][:r0]) for p in range(parts)], axis=0)
    wot[...] = tn(w_out, eye(heads * head_dim)).astype(BF16)

    span = half * WLON
    lat = (lax.broadcasted_iota(jnp.int32, (wtok, 1), 0) // WLON) % n_rows
    closed = (lat < half) if side == 0 else (lat >= half)
    shut = jnp.where(closed, penalty, 0.0)
    for p in range(parts):
        for h in range(heads_loc):
            rows = []
            for lev in range(levs):
                lo = n_a + h * wtok + lev * n_rows * WLON + q_row * WLON
                rows.append(a_parts[p][lo : lo + span].astype(F32))
            at = (p * heads_loc + h) * LANES
            bias[:, at : at + LANES] = (
                jnp.concatenate(rows * (LANES // qtok), axis=0).T * LOG2E + shut
            )

    first = lax.broadcasted_iota(jnp.int32, (1, LANES), 1) < qtok
    zero = jnp.zeros((), BF16)
    q_scale = head_dim**-0.5 * LOG2E
    e_all = heads * head_dim

    def zeros(rows):
        return jnp.zeros((rows, LANES), BF16)

    def attention(g):
        x = n_ref[g * GROUP : (g + 1) * GROUP]
        x_all = x.reshape(GROUP * wtok, feats)
        lo = q_row * WLON
        x_q = x.reshape(GROUP * levs, n_rows * WLON, feats)[:, lo : lo + span, :]
        k_all = nt(x_all, wk[...])
        v_all = nt(wv[...], x_all).astype(BF16)
        q_all = (nt(wq[...], x_q.reshape(GROUP * qtok, feats)) * q_scale).astype(BF16)
        mixed = []
        for pair in range(GROUP // 2):
            k0 = k_all[2 * pair * wtok : (2 * pair + 1) * wtok]
            k1 = k_all[(2 * pair + 1) * wtok : (2 * pair + 2) * wtok]
            q_t = q_all[:, pair * LANES : (pair + 1) * LANES]
            qa = jnp.where(first, q_t, zero)
            qb = jnp.where(first, zero, q_t)
            v_t = v_all[:, 2 * pair * wtok : (2 * pair + 2) * wtok]
            probs, inverse = [], []
            for e0 in range(0, e_all, LANES):
                dims = min(LANES, e_all - e0)
                if dims == LANES:
                    lhs = jnp.concatenate([k0[:, e0 : e0 + LANES], k1[:, e0 : e0 + LANES]], axis=1)
                else:
                    lhs = jnp.concatenate([k0[:, e0 : e0 + dims], k1[:, e0 : e0 + dims]], axis=1)
                columns = []
                for h in range(dims // head_dim):
                    a = e0 + h * head_dim
                    gaps = (h * head_dim, dims - (h + 1) * head_dim)
                    col = []
                    for q in (qa, qb):
                        if gaps[0]:
                            col.append(zeros(gaps[0]))
                        col.append(q[a : a + head_dim])
                        if gaps[1]:
                            col.append(zeros(gaps[1]))
                    columns.append(jnp.concatenate(col, axis=0))
                s = nn(lhs.astype(BF16), jnp.concatenate(columns, axis=1))
                for h in range(dims // head_dim):
                    at = (e0 // head_dim + h) * LANES
                    t = s[:, h * LANES : (h + 1) * LANES] + bias[:, at : at + LANES]
                    p = jnp.exp2(t - jnp.max(t, axis=0, keepdims=True))
                    inverse.append(1.0 / jnp.sum(p, axis=0, keepdims=True))
                    p = p.astype(BF16)
                    probs.append(
                        jnp.concatenate([jnp.where(first, p, zero), jnp.where(first, zero, p)], axis=0)
                    )
            out = []
            for h in range(0, heads, 2):
                o = nn(
                    v_t[h * head_dim : (h + 2) * head_dim],
                    jnp.concatenate(probs[h : h + 2], axis=1),
                )
                out.append(o[:head_dim, :LANES] * inverse[h])
                out.append(o[head_dim:, LANES:] * inverse[h + 1])
            mixed.append(jnp.concatenate(out, axis=0))
        mix = jnp.concatenate(mixed, axis=1).astype(BF16)
        at = g * GROUP * qtok
        return nn(wot[...], mix) + raw[:, at : at + GROUP * qtok].astype(F32)

    def feed_forward(g, s1):
        c = s1 - jnp.mean(s1, axis=0, keepdims=True)
        v = jnp.mean(c * c, axis=0, keepdims=True)
        n2 = (c * lax.rsqrt(v + 1e-05)).astype(BF16)
        total = s1
        step = 2 * LANES
        for i in range(0, ff_loc * parts, step):
            act = gelu(nn(wup[i : i + step], n2)).astype(BF16)
            total = total + nn(wdt[:, i : i + step], act)
        f = tn(total.astype(BF16), hw[...])
        for w in range(GROUP):
            at = (g * GROUP + w) * WLON
            fscr[:, :, at : at + WLON, :] = f[w * qtok : (w + 1) * qtok].reshape(
                levs, half, WLON, width
            )

    for g in range(windows // GROUP):
        feed_forward(g, attention(g))

    patches = half * (cols // dests)
    for lev in range(levs):
        f = fscr[lev].reshape(half * cols, width).astype(BF16)
        o = tn(f, perm[...]).astype(BF16)
        for d in range(dests):
            outs[d][lev] = o[:, d * patches : (d + 1) * patches]


def forecast(n_win, raw, hw, perm, a_parts, b_parts, *, side, dests, levs, n_rows, heads_loc):
    windows, wtok, feats = n_win.shape
    cols = windows * WLON
    half = n_rows // 2
    parts = len(a_parts)
    head_dim = feats // (heads_loc * parts)
    e_loc = heads_loc * head_dim
    width = hw.shape[1]
    ff_loc = (b_parts[0].shape[0] - e_loc * 3 // 2) * 2 * LANES // (3 * LANES + 2 * feats)
    heads = heads_loc * parts
    patches = half * (cols // dests)
    vm = pl.BlockSpec(memory_space=pltpu.VMEM)
    return pl.pallas_call(
        functools.partial(
            forecast_kernel,
            side=side,
            parts=parts,
            dests=dests,
            e_loc=e_loc,
            heads_loc=heads_loc,
            ff_loc=ff_loc,
            levs=levs,
            n_rows=n_rows,
        ),
        out_shape=[VMEM((levs, width, patches), BF16)] * dests,
        in_specs=[vm] * (4 + 2 * parts),
        out_specs=[vm] * dests,
        scratch_shapes=[
            pltpu.VMEM((feats, feats), BF16),
            pltpu.VMEM((feats, feats), BF16),
            pltpu.VMEM((feats, feats), BF16),
            pltpu.VMEM((feats, feats), BF16),
            pltpu.VMEM((ff_loc * parts, feats), BF16),
            pltpu.VMEM((feats, ff_loc * parts), BF16),
            pltpu.VMEM((wtok, heads * LANES), F32),
            pltpu.VMEM((levs, half, cols, width), F32),
        ],
        compiler_params=PARAMS,
    )(*map(near, (n_win, raw, hw, perm, *a_parts, *b_parts)))


def analysis_kernel(*refs, members, side):
    x_refs = refs[:members]
    idx, weight, value = refs[members : members + 3]
    out = refs[-1]
    levs, width, patches = x_refs[0].shape
    slots = idx.shape[1]
    half, cw = out.shape[2], out.shape[3]
    xs = [[x_refs[m][lev].astype(F32) for lev in range(levs)] for m in range(members)]
    state = lax.broadcasted_iota(jnp.int32, (width, patches), 0)
    pairs = [(i, k) for i in range(members) for k in range(i, members)]
    mat = {p: None for p in pairs}
    rhs = [None] * members
    for k in range(slots):
        at = idx[0, k : k + 1]
        hits = [state + lev * width == at for lev in range(levs)]
        y = []
        for m in range(members):
            total = jnp.where(hits[0], xs[m][0], 0.0)
            for lev in range(1, levs):
                total = jnp.where(hits[lev], xs[m][lev], total)
            y.append(jnp.sum(total, axis=0, keepdims=True))
        y_mean = sum(y[1:], y[0]) * (1.0 / members)
        yp = [v - y_mean for v in y]
        r = weight[0, k : k + 1]
        d = value[0, k : k + 1] - y_mean
        for i in range(members):
            ry = r * yp[i]
            for n in range(i, members):
                t = ry * yp[n]
                mat[i, n] = t if k == 0 else mat[i, n] + t
            t = ry * d
            rhs[i] = t if k == 0 else rhs[i] + t
    for i in range(members):
        mat[i, i] = mat[i, i] + (members - 1.0)
    trace = sum([mat[i, i] for i in range(1, members)], mat[0, 0])
    inv = 1.0 / trace

    def entry(a, i, n):
        return a[pairs.index((min(i, n), max(i, n)))]

    def times(a, b):
        res = []
        for i, n in pairs:
            acc = entry(a, i, 0) * entry(b, 0, n)
            for q in range(1, members):
                acc = acc + entry(a, i, q) * entry(b, q, n)
            res.append(acc)
        return res

    def sweep(_, carry):
        g, z = carry
        zg = times(z, g)
        f = [(1.5 if i == n else 0.0) - 0.5 * v for (i, n), v in zip(pairs, zg)]
        return times(g, f), times(f, z)

    g0 = [mat[p] * inv for p in pairs]
    z0 = [jnp.full_like(trace, 1.0 if i == n else 0.0) for i, n in pairs]
    _, z = lax.fori_loop(0, NEWTON, sweep, (g0, z0))
    zz = times(z, z)
    root = math.sqrt(members - 1.0) * lax.rsqrt(trace)
    mean_w = []
    for i in range(members):
        acc = entry(zz, i, 0) * rhs[0]
        for n in range(1, members):
            acc = acc + entry(zz, i, n) * rhs[n]
        mean_w.append(acc * inv)
    me = lax.axis_index("member")
    centers, spreads = [], []
    for lev in range(levs):
        total = xs[0][lev]
        for m in range(1, members):
            total = total + xs[m][lev]
        c = total * (1.0 / members)
        centers.append(c)
        spreads.append([xs[m][lev] - c for m in range(members)])
    for m in range(members):
        w = [mean_w[i] + root * entry(z, i, m) for i in range(members)]
        for lev in range(levs):
            acc = centers[lev]
            for i in range(members):
                acc = acc + spreads[lev][i] * w[i]
            out[m ^ me, lev] = acc.T.reshape(half, cw, width)


def analysis(xs, idx, weight, value, out_shape, side, prev):
    members = len(xs)
    levs, width, patches = xs[0].shape
    _, _, n_rows, cw, _ = out_shape
    half = n_rows // 2
    slots = idx.shape[1]
    vm = pl.BlockSpec(memory_space=pltpu.VMEM)
    obs = pl.BlockSpec((1, slots, patches), lambda i: (side, 0, 0))
    args = [*map(near, (*xs, idx, weight, value))]
    specs = [pl.BlockSpec((levs, width, patches), lambda i: (0, 0, 0))] * members + [obs] * 3
    aliases = {}
    if prev is not None:
        aliases = {len(args): 0}
        args.append(prev)
        specs.append(pl.BlockSpec(memory_space=pl.ANY))
    del vm
    return pl.pallas_call(
        functools.partial(analysis_kernel, members=members, side=side),
        grid=(1,),
        out_shape=jax.ShapeDtypeStruct(out_shape, F32),
        in_specs=specs,
        out_specs=pl.BlockSpec((members, levs, half, cw, width), lambda i: (0, 0, side, 0, 0)),
        input_output_aliases=aliases,
        compiler_params=PARAMS,
    )(*args)


def from_others(array, axis):
    size = lax.axis_size(axis)
    return [array] + [
        lax.ppermute(array, axis, [(i, (i + s) % size) for i in range(size)])
        for s in range(1, size)
    ]


def shards(
    prior_grids,
    w_qkv,
    w_out,
    w_up,
    w_down,
    head_weight,
    pos_bias,
    zonal_offsets,
    obs_index,
    obs_count,
    obs_value,
    obs_weight,
):
    member_grid = prior_grids[0]
    levs = member_grid.shape[0] // lax.axis_size("tensor")
    n_rows = member_grid.shape[1]
    dests = lax.axis_size("member")
    bands = lax.axis_size("band")
    heads_loc = pos_bias.shape[0]

    prior_t = member_grid.swapaxes(2, 3)
    half = n_rows // 2
    mine = lax.dynamic_slice_in_dim(prior_t, lax.axis_index("tensor") * levs, levs, 0)
    up = [(i, i + 1) for i in range(bands - 1)]
    above = lax.ppermute(mine[:, half:], "band", up)
    below = lax.ppermute(mine[:, :half], "band", [(b, a) for a, b in up])
    a_mine, b_mine = pack(w_qkv.transpose(1, 0, 2), w_out, w_up, w_down.T, pos_bias)
    a_parts = from_others(a_mine, "tensor")
    b_parts = from_others(b_mine, "tensor")
    obs = (
        obs_index[0].swapaxes(1, 2),
        obs_count[0],
        obs_value[0].swapaxes(1, 2),
        obs_weight[0].swapaxes(1, 2),
    )
    n_0, n_1, raw_0, raw_1, hw, perm, idx, value, weight = prologue(
        zonal_offsets, prior_t, above, below, head_weight.T, obs, levs, dests
    )
    cw = obs_index.shape[2]

    received = []
    for side, n_win, raw in ((0, n_0, raw_0), (1, n_1, raw_1)):
        if received:
            n_win, _ = lax.optimization_barrier((n_win, received[0][0]))
        sent = forecast(
            n_win,
            raw,
            hw,
            perm,
            a_parts,
            b_parts,
            side=side,
            dests=dests,
            levs=levs,
            n_rows=n_rows,
            heads_loc=heads_loc,
        )
        pieces = [sent[0]]
        for k in range(1, dests):
            pieces.append(lax.ppermute(sent[k], "member", [(i, i ^ k) for i in range(dests)]))
        received.append(pieces)
    out_shape = (dests, levs, n_rows, cw, head_weight.shape[1])
    result = None
    for side in range(2):
        result = analysis(received[side], idx, weight, value, out_shape, side, result)
    return result


def solution(mesh):
    return jax.shard_map(
        shards,
        mesh=mesh,
        in_specs=(
            P("member", None, "band", None, None),
            P(None, None, "tensor"),
            P("tensor", None),
            P(None, "tensor"),
            P("tensor", None),
            P(),
            P("tensor", None, None),
            P("member"),
            P("tensor", "band", "member", None),
            P("tensor", "band", "member"),
            P("tensor", "band", "member", None),
            P("tensor", "band", "member", None),
        ),
        out_specs=P(None, "tensor", "band", "member", None),
        check_vma=False,
    )
```

profile of v0, /device:TPU:0, one launch (start us, length us, event | category | flops | bytes accessed | tf_op | source)
XLA Modules:
  0.0 54.5 jit_solution(3791121931319703612)
XLA Ops:
  0.0 0.0 copy-start
  0.0 0.0 copy-start.1
  0.0 0.0 copy-start.9
  0.0 0.0 copy-start.4
  0.0 0.0 copy-start.5
  0.0 0.0 copy-start.6
  0.0 0.0 copy-start.10
  0.1 0.0 copy-start.7
  0.1 0.0 copy-start.8
  0.1 1.3 %dynamic-slice_bitcast_fusion = bf16[2,8,192,128]{3,2,1,0:T(8,128)(2,1)S(1)} fusion(bf16[1,4,8,128,192]{3,4,2,1,0:T(8,128)(2,1)} %param.12, s32[]{:T(128)S(6)} %select_n.3), kind=kLoop, calls=%fused_computation | loop fusion | bytes 1572868 | tf_op jit(solution)/shard_map/dynamic_slice | solution.py:547
  1.4 0.1 fusion
  1.5 2.4 %collective-permute-start = (bf16[2,4,192,128]{3,2,1,0:T(8,128)(2,1)S(1)}, bf16[2,4,192,128]{3,2,1,0:T(8,128)(2,1)S(1)}, u32[]{:S(2)}, u32[]{:S(2)}) collective-permute-start(bf16[2,4,192,128]{3,2,1,0:T(8,128)(2,1)S(1)} %get-tuple-element.46), channel_id=1, source_target_pairs={{0,2},{2,4},{4,6},{1,3},{3,5},{5,7},{8,10},{10,12},{12,14},{9,11},... | collective-permute-start | bytes 1179656 | tf_op jit(solution)/shard_map/ppermute | solution.py:549
  3.9 1.3 %collective-permute-start.1 = (bf16[2,4,192,128]{3,2,1,0:T(8,128)(2,1)S(1)}, bf16[2,4,192,128]{3,2,1,0:T(8,128)(2,1)S(1)}, u32[]{:S(2)}, u32[]{:S(2)}) collective-permute-start(bf16[2,4,192,128]{3,2,1,0:T(8,128)(2,1)S(1)} %get-tuple-element.45), channel_id=1, source_target_pairs={{2,0},{4,2},{6,4},{3,1},{5,3},{7,5},{10,8},{12,10},{14,12},{11,9},... | collective-permute-start | bytes 1179656 | tf_op jit(solution)/shard_map/ppermute | solution.py:550
  5.2 0.0 copy-done.1
  5.2 0.0 copy-done.9
  5.2 0.0 copy-done.2
  5.3 0.0 copy-done.3
  5.3 0.0 copy-done.4
  5.3 0.4 pack.1
  5.7 2.4 %collective-permute-start.3 = (bf16[1296,128]{1,0:T(8,128)(2,1)S(1)}, bf16[1296,128]{1,0:T(8,128)(2,1)S(1)}, u32[]{:S(2)}, u32[]{:S(2)}) collective-permute-start(bf16[1296,128]{1,0:T(8,128)(2,1)S(1)} %get-tuple-element.31.refs_6_), channel_id=1, source_target_pairs={{0,1},{1,0},{2,3},{3,2},{4,5},{5,4},{6,7},{7,6},{8,9},{9,8},{10,11... | collective-permute-start | bytes 995336 | tf_op jit(solution)/shard_map/ppermute | solution.py:519
  8.1 0.1 collective-permute-start.2
  8.8 0.0 collective-permute-done.above
  8.8 0.8 %collective-permute-done.1.below = bf16[2,4,192,128]{3,2,1,0:T(8,128)(2,1)S(1)} collective-permute-done((bf16[2,4,192,128]{3,2,1,0:T(8,128)(2,1)S(1)}, bf16[2,4,192,128]{3,2,1,0:T(8,128)(2,1)S(1)}, u32[]{:S(2)}, u32[]{:S(2)}) %collective-permute-start.1) | collective-permute-done | bytes 393248 | tf_op jit(solution)/shard_map/ppermute | solution.py:550
  9.6 0.0 copy-done
  9.6 0.0 copy-done.5
  9.7 0.0 copy-done.6
  9.7 0.0 copy-done.10
  9.7 0.0 copy-done.7
  9.7 0.0 copy-done.8
  9.7 3.7 %prologue.1 = (bf16[16,128,192]{2,1,0:T(8,128)(2,1)S(1)}, bf16[16,128,192]{2,1,0:T(8,128)(2,1)S(1)}, bf16[192,1024]{1,0:T(8,128)(2,1)S(1)}, bf16[192,1024]{1,0:T...) custom-call(s32[1]{0:T(128)S(6)} %copy.15.offs, ...), custom_call_target="tpu_custom_call" | custom-call | tf_op jit(solution)/shard_map/prologue/pallas_call | solution.py:188
  13.3 6.0 %collective-permute-done.2.refs_5_ = bf16[816,128]{1,0:T(8,128)(2,1)S(1)} collective-permute-done((bf16[816,128]{1,0:T(8,128)(2,1)S(1)}, bf16[816,128]{1,0:T(8,128)(2,1)S(1)}, u32[]{:S(2)}, u32[]{:S(2)}) %collective-permute-start.2) | collective-permute-done | bytes 208928 | tf_op jit(solution)/shard_map/ppermute | solution.py:519
  19.3 0.0 collective-permute-done.3.refs_7_
  19.3 8.1 %shard_map.118 = (bf16[2,160,128]{2,1,0:T(8,128)(2,1)S(1)}, bf16[2,160,128]{2,1,0:T(8,128)(2,1)S(1)}, bf16[2,160,128]{2,1,0:T(8,128)(2,1)S(1)}, bf16[2,160,128]{2,1,0:T(8,128)(2,1)S(1)}) custom-call(bf16[16,128,192]{2,1,0:T(8,128)(2,1)S(1)} %get-tuple-element.26.refs_0_, bf16[192,1024]{1,0:T(8,128)(2,1)S(1)} %get-tuple-element.27.refs_1_, ...), custom_call_target="tpu_custom_call" | custom-call | tf_op jit(solution)/shard_map/pallas_call | solution.py:376
  27.4 2.6 %collective-permute-start.7 = (bf16[2,160,128]{2,1,0:T(8,128)(2,1)S(1)}, bf16[2,160,128]{2,1,0:T(8,128)(2,1)S(1)}, u32[]{:S(2)}, u32[]{:S(2)}) collective-permute-start(bf16[2,160,128]{2,1,0:T(8,128)(2,1)S(1)} %get-tuple-element.42), channel_id=1, source_target_pairs={{0,8},{8,0},{16,24},{24,16},{1,9},{9,1},{17,25},{25,17},{2,10},{10... | collective-permute-start | bytes 245768 | tf_op jit(solution)/shard_map/ppermute | solution.py:584
  30.0 2.6 %collective-permute-start.8 = (bf16[2,160,128]{2,1,0:T(8,128)(2,1)S(1)}, bf16[2,160,128]{2,1,0:T(8,128)(2,1)S(1)}, u32[]{:S(2)}, u32[]{:S(2)}) collective-permute-start(bf16[2,160,128]{2,1,0:T(8,128)(2,1)S(1)} %get-tuple-element.43), channel_id=1, source_target_pairs={{0,16},{8,24},{16,0},{24,8},{1,17},{9,25},{17,1},{25,9},{2,18},{10... | collective-permute-start | bytes 245768 | tf_op jit(solution)/shard_map/ppermute | solution.py:584
  32.6 0.0 collective-permute-start.9
  32.6 8.1 %shard_map.119 = (bf16[2,160,128]{2,1,0:T(8,128)(2,1)S(1)}, bf16[2,160,128]{2,1,0:T(8,128)(2,1)S(1)}, bf16[2,160,128]{2,1,0:T(8,128)(2,1)S(1)}, bf16[2,160,128]{2,1,0:T(8,128)(2,1)S(1)}) custom-call(bf16[16,128,192]{2,1,0:T(8,128)(2,1)S(1)} %get-tuple-element.33.refs_0_, bf16[192,1024]{1,0:T(8,128)(2,1)S(1)} %get-tuple-element.34.refs_1_, ...), custom_call_target="tpu_custom_call" | custom-call | tf_op jit(solution)/shard_map/pallas_call | solution.py:376
  40.7 1.0 %collective-permute-start.4 = (bf16[2,160,128]{2,1,0:T(8,128)(2,1)S(1)}, bf16[2,160,128]{2,1,0:T(8,128)(2,1)S(1)}, u32[]{:S(2)}, u32[]{:S(2)}) collective-permute-start(bf16[2,160,128]{2,1,0:T(8,128)(2,1)S(1)} %get-tuple-element.36), channel_id=1, source_target_pairs={{0,8},{8,0},{16,24},{24,16},{1,9},{9,1},{17,25},{25,17},{2,10},{10... | collective-permute-start | bytes 245768 | tf_op jit(solution)/shard_map/ppermute | solution.py:584
  41.7 3.5 %collective-permute-start.5 = (bf16[2,160,128]{2,1,0:T(8,128)(2,1)S(1)}, bf16[2,160,128]{2,1,0:T(8,128)(2,1)S(1)}, u32[]{:S(2)}, u32[]{:S(2)}) collective-permute-start(bf16[2,160,128]{2,1,0:T(8,128)(2,1)S(1)} %get-tuple-element.37), channel_id=1, source_target_pairs={{0,16},{8,24},{16,0},{24,8},{1,17},{9,25},{17,1},{25,9},{2,18},{10... | collective-permute-start | bytes 245768 | tf_op jit(solution)/shard_map/ppermute | solution.py:584
  45.2 0.0 collective-permute-done.7.refs_1_
  45.2 0.0 collective-permute-start.6
  45.2 0.0 collective-permute-done.8.refs_2_
  45.2 0.0 collective-permute-done.9.refs_3_
  45.2 2.8 %shard_map.120.refs_7_ = f32[4,2,8,32,160]{4,3,2,1,0:T(8,128)} custom-call(bf16[2,160,128]{2,1,0:T(8,128)(2,1)S(1)} %get-tuple-element.32.refs_0_, bf16[2,160,128]{2,1,0:T(8,128)(2,1)S(1)} %collective-permute-done.7.refs_1_, bf16[2,160,128]{2,1,0:T(8,128)(2,1)S(1)} %collective-permute-done.8.refs_2_, ...), custom_call_target="tpu_custom_call" | custom-call | tf_op jit(solution)/shard_map/pallas_call | solution.py:505
  48.0 0.0 collective-permute-done.4.refs_1_
  48.0 4.0 %collective-permute-done.5.refs_2_ = bf16[2,160,128]{2,1,0:T(8,128)(2,1)S(1)} collective-permute-done((bf16[2,160,128]{2,1,0:T(8,128)(2,1)S(1)}, bf16[2,160,128]{2,1,0:T(8,128)(2,1)S(1)}, u32[]{:S(2)}, u32[]{:S(2)}) %collective-permute-start.5) | collective-permute-done | bytes 81952 | tf_op jit(solution)/shard_map/ppermute | solution.py:584
  51.9 0.0 collective-permute-done.6.refs_3_
  52.0 2.6 %shard_map.121 = f32[4,2,8,32,160]{4,3,2,1,0:T(8,128)} custom-call(bf16[2,160,128]{2,1,0:T(8,128)(2,1)S(1)} %get-tuple-element.35.refs_0_, bf16[2,160,128]{2,1,0:T(8,128)(2,1)S(1)} %collective-permute-done.4.refs_1_, bf16[2,160,128]{2,1,0:T(8,128)(2,1)S(1)} %collective-permute-done.5.refs_2_, ...), custom_call_target="tpu_custom_call", output_to_operand_aliasing={{}: (7, {})} | custom-call | tf_op jit(solution)/shard_map/pallas_call | solution.py:505
  (2 shorter events, 0.0 us)
Async XLA Ops:
  0.0 9.6 %copy-start = (bf16[1,4,8,128,192]{3,4,2,1,0:T(8,128)(2,1)S(1)}, bf16[1,4,8,128,192]{3,4,2,1,0:T(8,128)(2,1)}, u32[]{:S(2)}) copy-start(bf16[1,4,8,128,192]{3,4,2,1,0:T(8,128)(2,1)} %param.12) | copy-start | bytes 4718596
  0.0 5.2 %copy-start.1 = (bf16[192,3,96]{2,0,1:T(8,128)(2,1)S(1)}, bf16[192,3,96]{2,0,1:T(8,128)(2,1)}, u32[]{:S(2)}) copy-start(bf16[192,3,96]{2,0,1:T(8,128)(2,1)} %param.13) | copy-start | bytes 331780
  0.0 5.2 %copy-start.9 = (bf16[96,192]{1,0:T(8,128)(2,1)S(1)}, bf16[96,192]{1,0:T(8,128)(2,1)}, u32[]{:S(2)}) copy-start(bf16[96,192]{1,0:T(8,128)(2,1)} %w_out.1) | copy-start | bytes 110596
  0.0 5.2 %copy-start.2 = (bf16[192,384]{1,0:T(8,128)(2,1)S(1)}, bf16[192,384]{1,0:T(8,128)(2,1)}, u32[]{:S(2)}) copy-start(bf16[192,384]{1,0:T(8,128)(2,1)} %w_up.1) | copy-start | bytes 442372
  0.0 5.3 %copy-start.3 = (bf16[384,192]{0,1:T(8,128)(2,1)S(1)}, bf16[384,192]{0,1:T(8,128)(2,1)}, u32[]{:S(2)}) copy-start(bf16[384,192]{0,1:T(8,128)(2,1)} %param.16) | copy-start | bytes 442372
  0.0 5.3 %copy-start.4 = (bf16[3,128,128]{2,1,0:T(8,128)(2,1)S(1)}, bf16[3,128,128]{2,1,0:T(8,128)(2,1)}, u32[]{:S(2)}) copy-start(bf16[3,128,128]{2,1,0:T(8,128)(2,1)} %bias.1) | copy-start | bytes 294916
  0.0 9.6 %copy-start.5 = (bf16[192,160]{0,1:T(8,128)(2,1)S(1)}, bf16[192,160]{0,1:T(8,128)(2,1)}, u32[]{:S(2)}) copy-start(bf16[192,160]{0,1:T(8,128)(2,1)} %param.17) | copy-start | bytes 184324
  0.0 9.6 %copy-start.6 = (s32[1,8,32,16]{2,3,1,0:T(8,128)S(1)}, s32[1,8,32,16]{2,3,1,0:T(8,128)}, u32[]{:S(2)}) copy-start(s32[1,8,32,16]{2,3,1,0:T(8,128)} %param.20) | copy-start | bytes 49156
  0.0 9.6 %copy-start.10 = (s32[1,8,32]{2,1,0:T(8,128)S(1)}, s32[1,8,32]{2,1,0:T(8,128)}, u32[]{:S(2)}) copy-start(s32[1,8,32]{2,1,0:T(8,128)} %param.21) | copy-start | bytes 3076
  0.1 9.6 %copy-start.7 = (f32[1,8,32,16]{2,3,1,0:T(8,128)S(1)}, f32[1,8,32,16]{2,3,1,0:T(8,128)}, u32[]{:S(2)}) copy-start(f32[1,8,32,16]{2,3,1,0:T(8,128)} %param.22) | copy-start | bytes 49156
  0.1 9.6 %copy-start.8 = (f32[1,8,32,16]{2,3,1,0:T(8,128)S(1)}, f32[1,8,32,16]{2,3,1,0:T(8,128)}, u32[]{:S(2)}) copy-start(f32[1,8,32,16]{2,3,1,0:T(8,128)} %param.23) | copy-start | bytes 49156
  1.5 7.3 %collective-permute-start = (bf16[2,4,192,128]{3,2,1,0:T(8,128)(2,1)S(1)}, bf16[2,4,192,128]{3,2,1,0:T(8,128)(2,1)S(1)}, u32[]{:S(2)}, u32[]{:S(2)}) collective-permute-start(bf16[2,4,192,128]{3,2,1,0:T(8,128)(2,1)S(1)} %get-tuple-element.46), channel_id=1, source_target_pairs={{0,2},{2,4},{4,6},{1,3},{3,5},{5,7},{8,10},{10,12},{12,14},{9,11},... | collective-permute-start | bytes 1179656 | tf_op jit(solution)/shard_map/ppermute | solution.py:549
  3.9 5.7 %collective-permute-start.1 = (bf16[2,4,192,128]{3,2,1,0:T(8,128)(2,1)S(1)}, bf16[2,4,192,128]{3,2,1,0:T(8,128)(2,1)S(1)}, u32[]{:S(2)}, u32[]{:S(2)}) collective-permute-start(bf16[2,4,192,128]{3,2,1,0:T(8,128)(2,1)S(1)} %get-tuple-element.45), channel_id=1, source_target_pairs={{2,0},{4,2},{6,4},{3,1},{5,3},{7,5},{10,8},{12,10},{14,12},{11,9},... | collective-permute-start | bytes 1179656 | tf_op jit(solution)/shard_map/ppermute | solution.py:550
  5.7 13.6 %collective-permute-start.3 = (bf16[1296,128]{1,0:T(8,128)(2,1)S(1)}, bf16[1296,128]{1,0:T(8,128)(2,1)S(1)}, u32[]{:S(2)}, u32[]{:S(2)}) collective-permute-start(bf16[1296,128]{1,0:T(8,128)(2,1)S(1)} %get-tuple-element.31.refs_6_), channel_id=1, source_target_pairs={{0,1},{1,0},{2,3},{3,2},{4,5},{5,4},{6,7},{7,6},{8,9},{9,8},{10,11... | collective-permute-start | bytes 995336 | tf_op jit(solution)/shard_map/ppermute | solution.py:519
  8.1 11.2 %collective-permute-start.2 = (bf16[816,128]{1,0:T(8,128)(2,1)S(1)}, bf16[816,128]{1,0:T(8,128)(2,1)S(1)}, u32[]{:S(2)}, u32[]{:S(2)}) collective-permute-start(bf16[816,128]{1,0:T(8,128)(2,1)S(1)} %get-tuple-element.30.refs_4_), channel_id=1, source_target_pairs={{0,1},{1,0},{2,3},{3,2},{4,5},{5,4},{6,7},{7,6},{8,9},{9,8},{10,11... | collective-permute-start | bytes 626696 | tf_op jit(solution)/shard_map/ppermute | solution.py:519
  27.4 17.8 %collective-permute-start.7 = (bf16[2,160,128]{2,1,0:T(8,128)(2,1)S(1)}, bf16[2,160,128]{2,1,0:T(8,128)(2,1)S(1)}, u32[]{:S(2)}, u32[]{:S(2)}) collective-permute-start(bf16[2,160,128]{2,1,0:T(8,128)(2,1)S(1)} %get-tuple-element.42), channel_id=1, source_target_pairs={{0,8},{8,0},{16,24},{24,16},{1,9},{9,1},{17,25},{25,17},{2,10},{10... | collective-permute-start | bytes 245768 | tf_op jit(solution)/shard_map/ppermute | solution.py:584
  30.0 15.1 %collective-permute-start.8 = (bf16[2,160,128]{2,1,0:T(8,128)(2,1)S(1)}, bf16[2,160,128]{2,1,0:T(8,128)(2,1)S(1)}, u32[]{:S(2)}, u32[]{:S(2)}) collective-permute-start(bf16[2,160,128]{2,1,0:T(8,128)(2,1)S(1)} %get-tuple-element.43), channel_id=1, source_target_pairs={{0,16},{8,24},{16,0},{24,8},{1,17},{9,25},{17,1},{25,9},{2,18},{10... | collective-permute-start | bytes 245768 | tf_op jit(solution)/shard_map/ppermute | solution.py:584
  32.6 12.6 %collective-permute-start.9 = (bf16[2,160,128]{2,1,0:T(8,128)(2,1)S(1)}, bf16[2,160,128]{2,1,0:T(8,128)(2,1)S(1)}, u32[]{:S(2)}, u32[]{:S(2)}) collective-permute-start(bf16[2,160,128]{2,1,0:T(8,128)(2,1)S(1)} %get-tuple-element.44), channel_id=1, source_target_pairs={{0,24},{8,16},{16,8},{24,0},{1,25},{9,17},{17,9},{25,1},{2,26},{10... | collective-permute-start | bytes 245768 | tf_op jit(solution)/shard_map/ppermute | solution.py:584
  40.7 7.3 %collective-permute-start.4 = (bf16[2,160,128]{2,1,0:T(8,128)(2,1)S(1)}, bf16[2,160,128]{2,1,0:T(8,128)(2,1)S(1)}, u32[]{:S(2)}, u32[]{:S(2)}) collective-permute-start(bf16[2,160,128]{2,1,0:T(8,128)(2,1)S(1)} %get-tuple-element.36), channel_id=1, source_target_pairs={{0,8},{8,0},{16,24},{24,16},{1,9},{9,1},{17,25},{25,17},{2,10},{10... | collective-permute-start | bytes 245768 | tf_op jit(solution)/shard_map/ppermute | solution.py:584
  41.7 10.3 %collective-permute-start.5 = (bf16[2,160,128]{2,1,0:T(8,128)(2,1)S(1)}, bf16[2,160,128]{2,1,0:T(8,128)(2,1)S(1)}, u32[]{:S(2)}, u32[]{:S(2)}) collective-permute-start(bf16[2,160,128]{2,1,0:T(8,128)(2,1)S(1)} %get-tuple-element.37), channel_id=1, source_target_pairs={{0,16},{8,24},{16,0},{24,8},{1,17},{9,25},{17,1},{25,9},{2,18},{10... | collective-permute-start | bytes 245768 | tf_op jit(solution)/shard_map/ppermute | solution.py:584
  45.2 6.8 %collective-permute-start.6 = (bf16[2,160,128]{2,1,0:T(8,128)(2,1)S(1)}, bf16[2,160,128]{2,1,0:T(8,128)(2,1)S(1)}, u32[]{:S(2)}, u32[]{:S(2)}) collective-permute-start(bf16[2,160,128]{2,1,0:T(8,128)(2,1)S(1)} %get-tuple-element.38), channel_id=1, source_target_pairs={{0,24},{8,16},{16,8},{24,0},{1,25},{9,17},{17,9},{25,1},{2,26},{10... | collective-permute-start | bytes 245768 | tf_op jit(solution)/shard_map/ppermute | solution.py:584
where the time goes:
time: 54.7 us; the launch traced here: 54.5 us
  Pallas kernels  25.6 us (47%)
  starting transfers between devices  15.9 us (29%)
  waiting for transfers between devices  10.8 us (20%)
  local copies, waits for them, and re-layouts  1.44 us (3%)
  between operations  0.86 us (2%)
    pallas_call x2, Pallas kernels, forecast(): pl.pallas_call(functools.partial(forecast_kernel, side=side, parts=parts,...  16.2 us
    ppermute x6, starting transfers between devices, shards(): lax.ppermute(sent[k], 'member', [(i, i ^ k) for i in range(dests)])  9.68 us
    ppermute x2, waiting for transfers between devices, from_others(): lax.ppermute(array, axis, [(i, (i + s) % size) for i in range(size)])  5.98 us
    pallas_call x2, Pallas kernels, analysis(): pl.pallas_call(functools.partial(analysis_kernel, members=members, side=s...  5.36 us
    ppermute x6, waiting for transfers between devices, shards(): lax.ppermute(sent[k], 'member', [(i, i ^ k) for i in range(dests)])  3.98 us
    pallas_call x1, Pallas kernels, prologue(): pl.pallas_call(prologue_kernel, out_shape=(n_shape, n_shape, raw_shape, r...  3.65 us
    ppermute x2, starting transfers between devices, from_others(): lax.ppermute(array, axis, [(i, (i + s) % size) for i in range(size)])  2.45 us
    ppermute x1, starting transfers between devices, shards(): above = lax.ppermute(mine[:, half:], 'band', up)  2.43 us
  transfers between devices with their start and end apart: 10, of which 3 were waited for; matrix products, arithmetic and copies ran while one was open for 0% of the time, Pallas kernels for 27%

commit v1 on v0

--- a/solution.py
+++ b/solution.py
@@ -26,6 +26,10 @@
     return pltpu.with_memory_space_constraint(x, pltpu.VMEM)
 
 
+def far(x):
+    return pltpu.with_memory_space_constraint(x, pltpu.HBM)
+
+
 def nn(a, b):
     return lax.dot_general(a, b, (((1,), (0,)), ((), ())), preferred_element_type=F32)
 
@@ -60,50 +64,99 @@
     return jnp.concatenate([d[:rows], high], axis=1)
 
 
-def pack_kernel(qkv, w_out, w_up, w_down, bias, a_ref, b_ref):
+def pack_kernel(prior, *refs):
+    weights, (full, half, own, top, bot), (*local, sems) = refs[:5], refs[5:10], refs[10:]
+    levs, n_rows, feats, _ = own.shape
+    mid = n_rows // 2
+    here = pl.ds(lax.axis_index("tensor") * levs, levs)
+    loads = [
+        pltpu.make_async_copy(src, dst, sems.at[i])
+        for i, (src, dst) in enumerate(zip(weights, local))
+    ]
+    copies = [
+        pltpu.make_async_copy(prior.at[here, :mid], top, sems.at[5]),
+        pltpu.make_async_copy(prior.at[here, mid:], bot, sems.at[6]),
+        pltpu.make_async_copy(prior.at[here], own, sems.at[7]),
+    ]
+    for copy in loads + copies:
+        copy.start()
+    for copy in loads:
+        copy.wait()
+    qkv, w_out, w_up, w_down, bias = local
     ident = eye(qkv.shape[2])
     dense = to_dense(jnp.concatenate([nt(ident, qkv[i]).astype(BF16) for i in range(3)], axis=0))
-    n_a = dense.shape[0]
-    a_ref[:n_a] = dense
+    at = dense.shape[0]
+    full[:at] = dense
     heads, wtok, _ = bias.shape
     for h in range(heads):
-        a_ref[n_a + h * wtok : n_a + (h + 1) * wtok] = bias[h]
-    o = to_dense(w_out[...])
-    r0 = o.shape[0]
-    b_ref[:r0] = o
-    up = to_dense(nt(eye(w_up.shape[1]), w_up[...]).astype(BF16))
-    r1 = r0 + up.shape[0]
-    b_ref[r0:r1] = up
-    feats, ff = w_down.shape
-    for i in range(ff // LANES):
-        b_ref[r1 + i * feats : r1 + (i + 1) * feats] = w_down[:, i * LANES : (i + 1) * LANES]
-
-
-def pack(qkv, w_out, w_up, w_down, bias):
-    _, feats, e_loc = qkv.shape
+        full[at + h * wtok : at + (h + 1) * wtok] = bias[h]
+    at += heads * wtok
+    for piece in (to_dense(w_out[...]), to_dense(nt(eye(w_up.shape[1]), w_up[...]).astype(BF16))):
+        full[at : at + piece.shape[0]] = piece
+        at += piece.shape[0]
+    for i in range(w_down.shape[1] // LANES):
+        full[at : at + feats] = w_down[:, i * LANES : (i + 1) * LANES]
+        at += feats
+    rows = half.shape[0]
+    mine = lax.axis_index("band") % 2
+    half[...] = full[pl.ds(pl.multiple_of(mine * rows, 16), rows)]
+    for copy in copies:
+        copy.wait()
+
+
+def pack(prior_t, qkv, w_out, w_up, w_down, bias, levs):
+    _, n_rows, feats, cols = prior_t.shape
+    e_loc = qkv.shape[2]
     heads, wtok, _ = bias.shape
     ff = w_up.shape[1]
-    a_rows = 3 * e_loc * 3 // 2 + heads * wtok
-    b_rows = e_loc * 3 // 2 + ff * 3 // 2 + feats * (ff // LANES)
+    rows = 3 * e_loc * 3 // 2 + heads * wtok + e_loc * 3 // 2 + ff * 3 // 2 + feats * (ff // LANES)
     vm = pl.BlockSpec(memory_space=pltpu.VMEM)
+    edge = VMEM((levs, n_rows // 2, feats, cols), BF16)
     return pl.pallas_call(
         pack_kernel,
-        out_shape=(VMEM((a_rows, LANES), BF16), VMEM((b_rows, LANES), BF16)),
-        in_specs=[vm] * 5,
-        out_specs=[vm] * 2,
+        out_shape=(
+            VMEM((rows, LANES), BF16),
+            VMEM((rows // 2, LANES), BF16),
+            VMEM((levs, n_rows, feats, cols), BF16),
+            edge,
+            edge,
+        ),
+        in_specs=[pl.BlockSpec(memory_space=pltpu.HBM)] * 6,
+        out_specs=[vm] * 5,
+        scratch_shapes=[VMEM(w.shape, BF16) for w in (qkv, w_out, w_up, w_down, bias)]
+        + [pltpu.SemaphoreType.DMA((8,))],
         compiler_params=PARAMS,
         name="pack",
-    )(qkv, w_out, w_up, w_down, bias)
-
-
-def prologue_kernel(offs, prior, above, below, hw_t, obs_i, obs_n, obs_v, obs_w, *refs):
-    n_refs, raw_refs, hw, perm, idx, val, wgt, own, xscr, sem = refs[:2], refs[2:4], *refs[4:]
+    )(*map(far, (prior_t, qkv, w_out, w_up, w_down, bias)))
+
+
+def roll_matrix(off, cols):
+    j = lax.broadcasted_iota(jnp.int32, (cols, cols), 0) + off
+    j = jnp.where(j >= cols, j - cols, j)
+    return (j == lax.broadcasted_iota(jnp.int32, (cols, cols), 1)).astype(BF16)
+
+
+def norm_rows(x):
+    feats = x.shape[0]
+    x = x.astype(F32)
+    c = x - jnp.sum(x, axis=0, keepdims=True) * (1.0 / feats)
+    v = jnp.sum(c * c, axis=0, keepdims=True) * (1.0 / feats)
+    return (c * lax.rsqrt(v + 1e-05)).astype(BF16)
+
+
+def by_window(first, second):
+    cols, feats = first.shape
+    f = first.reshape(cols // WLON, 1, WLON, feats)
+    s = second.reshape(cols // WLON, 1, WLON, feats)
+    both = jnp.concatenate([f, s], axis=1)
+    return both.reshape(cols // WLON, 2 * WLON, feats).astype(BF16)
+
+
+def own_kernel(offs, own, hw_t, obs_i, obs_n, obs_v, obs_w, *refs):
+    n_refs, raw_refs, hw, perm, idx, val, wgt, xscr = refs[:2], refs[2:4], *refs[4:]
     levs, n_rows, feats, cols = own.shape
     half = n_rows // 2
     windows = cols // WLON
-    start = lax.axis_index("tensor") * levs
-    copy = pltpu.make_async_copy(prior.at[pl.ds(start, levs)], own, sem)
-    copy.start()
     off = offs[0]
     me = lax.axis_index("member")
     dests = lax.axis_size("member")
@@ -117,10 +170,6 @@
         wgt[side] = jnp.concatenate(
             [jnp.where(slot < obs_n[r : r + 1], obs_w[r], 0.0) for r in at], axis=1
         )
-
-    j = lax.broadcasted_iota(jnp.int32, (cols, cols), 0) + off
-    j = jnp.where(j >= cols, j - cols, j)
-    rollm = (j == lax.broadcasted_iota(jnp.int32, (cols, cols), 1)).astype(BF16)
 
     cw = cols // dests
     patches = half * cw
@@ -134,59 +183,40 @@
             hit = base + r * cw == lane + b * LANES
             perm[r * cols : (r + 1) * cols, b * LANES : (b + 1) * LANES] = hit.astype(BF16)
 
-    def norm(x):
-        x = x.astype(F32)
-        c = x - jnp.sum(x, axis=0, keepdims=True) * (1.0 / feats)
-        v = jnp.sum(c * c, axis=0, keepdims=True) * (1.0 / feats)
-        return (c * lax.rsqrt(v + 1e-05)).astype(BF16)
-
-    def by_window(first, second):
-        f = first.reshape(windows, 1, WLON, feats)
-        s = second.reshape(windows, 1, WLON, feats)
-        return jnp.concatenate([f, s], axis=1).reshape(windows, 2 * WLON, feats).astype(BF16)
-
-    copy.wait()
+    rollm = roll_matrix(off, cols)
+    qtok = levs * half * WLON
+    ident = eye(feats)
     for side in range(2):
-        halo = (above, below)[side]
-
-        def one_level(lev, carry, side=side, halo=halo):
+
+        def one_level(lev, carry, side=side):
             for r in range(0, half, 2):
                 x0, x1 = own[lev, side * half + r], own[lev, side * half + r + 1]
-                own_row = half + r if side == 0 else r
-                at = pl.multiple_of(lev * (n_rows * WLON) + own_row * WLON, 2 * WLON)
-                n_refs[side][:, pl.ds(at, 2 * WLON), :] = by_window(
-                    nt(rollm, norm(x0)), nt(rollm, norm(x1))
+                n_refs[side][:, lev, r * WLON : (r + 2) * WLON, :] = by_window(
+                    nt(rollm, norm_rows(x0)), nt(rollm, norm_rows(x1))
                 )
-                at = pl.multiple_of(lev * (half * WLON) + r * WLON, 2 * WLON)
-                xscr[:, pl.ds(at, 2 * WLON), :] = by_window(nt(rollm, x0), nt(rollm, x1))
-                h0, h1 = halo[lev, r], halo[lev, r + 1]
-                halo_row = r if side == 0 else half + r
-                at = pl.multiple_of(lev * (n_rows * WLON) + halo_row * WLON, 2 * WLON)
-                n_refs[side][:, pl.ds(at, 2 * WLON), :] = by_window(
-                    nt(rollm, norm(h0)), nt(rollm, norm(h1))
+                xscr[:, lev, r * WLON : (r + 2) * WLON, :] = by_window(
+                    nt(rollm, x0), nt(rollm, x1)
                 )
             return carry
 
         lax.fori_loop(0, levs, one_level, 0)
-        qtok = levs * half * WLON
-        ident = eye(feats)
         for w in range(0, windows, GROUP):
             x = xscr[w : w + GROUP].reshape(GROUP * qtok, feats)
             raw_refs[side][:, w * qtok : (w + GROUP) * qtok] = nt(ident, x).astype(BF16)
 
 
-def prologue(offs, prior_t, above, below, hw_t, obs, levs, dests):
+def prepare_own(offs, own, hw_t, obs, dests):
+    levs, n_rows, feats, cols = own.shape
     slots = obs[0].shape[1]
-    patches = prior_t.shape[1] // 2 * (prior_t.shape[3] // dests)
-    _, n_rows, feats, cols = prior_t.shape
     half = n_rows // 2
+    patches = half * (cols // dests)
     windows = cols // WLON
     width = hw_t.shape[0]
-    n_shape = VMEM((windows, levs * n_rows * WLON, feats), BF16)
+    n_shape = VMEM((windows, levs, half * WLON, feats), BF16)
     raw_shape = VMEM((feats, levs * half * cols), BF16)
     vm = pl.BlockSpec(memory_space=pltpu.VMEM)
     return pl.pallas_call(
-        prologue_kernel,
+        own_kernel,
         out_shape=(
             n_shape,
             n_shape,
@@ -198,32 +228,51 @@
             VMEM((2, slots, patches), F32),
             VMEM((2, slots, patches), F32),
         ),
-        in_specs=[pl.BlockSpec(memory_space=pltpu.SMEM), pl.BlockSpec(memory_space=pl.ANY)]
-        + [vm] * 7,
+        in_specs=[pl.BlockSpec(memory_space=pltpu.SMEM)] + [vm] * 6,
         out_specs=[vm] * 9,
-        scratch_shapes=[
-            pltpu.VMEM((levs, n_rows, feats, cols), BF16),
-            pltpu.VMEM((windows, levs * half * WLON, feats), BF16),
-            pltpu.SemaphoreType.DMA,
-        ],
+        scratch_shapes=[VMEM(n_shape.shape, BF16)],
         compiler_params=PARAMS,
-        name="prologue",
-    )(offs, prior_t, near(above), near(below), hw_t, *obs)
-
-
-def gelu(x):
-    return 0.5 * x * (1.0 + lax.erf(x * math.sqrt(0.5)))
-
-
-def forecast_kernel(*refs, side, parts, dests, e_loc, heads_loc, ff_loc, levs, n_rows):
-    n_ref, raw, hw, perm = refs[:4]
-    a_parts = refs[4 : 4 + parts]
-    b_parts = refs[4 + parts : 4 + 2 * parts]
-    refs = refs[4 + 2 * parts :]
-    outs = refs[:dests]
-    (wq, wk, wv, wot, wup, wdt, bias, fscr) = refs[dests:]
-    windows, wtok, feats = n_ref.shape
-    half = n_rows // 2
+        name="prepare_own",
+    )(offs, near(own), near(hw_t), *map(near, obs))
+
+
+def halo_kernel(offs, above, below, *n_refs):
+    levs, half, _, cols = above.shape
+    rollm = roll_matrix(offs[0], cols)
+    for side, halo in enumerate((above, below)):
+
+        def one_level(lev, carry, side=side, halo=halo):
+            for r in range(0, half, 2):
+                n_refs[side][:, lev, r * WLON : (r + 2) * WLON, :] = by_window(
+                    nt(rollm, norm_rows(halo[lev, r])), nt(rollm, norm_rows(halo[lev, r + 1]))
+                )
+            return carry
+
+        lax.fori_loop(0, levs, one_level, 0)
+
+
+def prepare_halo(offs, above, below):
+    levs, half, feats, cols = above.shape
+    vm = pl.BlockSpec(memory_space=pltpu.VMEM)
+    return pl.pallas_call(
+        halo_kernel,
+        out_shape=[VMEM((cols // WLON, levs, half * WLON, feats), BF16)] * 2,
+        in_specs=[pl.BlockSpec(memory_space=pltpu.SMEM), vm, vm],
+        out_specs=[vm] * 2,
+        compiler_params=PARAMS,
+        name="prepare_halo",
+    )(offs, near(above), near(below))
+
+
+def forecast_kernel(*refs, side, dests, e_loc, heads_loc, ff_loc):
+    n_halo, n_own, raw, hw, perm, mine, got, passed = refs[:8]
+    outs = refs[8 : 8 + dests]
+    (wq, wk, wv, wot, wup, wdt, bias, fscr, theirs) = refs[8 + dests :]
+    windows, levs, span, feats = n_own.shape
+    half = span // WLON
+    n_rows = 2 * half
+    wtok = levs * n_rows * WLON
+    parts = 2
     cols = windows * WLON
     qtok = levs * half * WLON
     heads = heads_loc * parts
@@ -237,23 +286,28 @@
         is_open = band < lax.axis_size("band") - 1
     penalty = jnp.where(is_open, 0.0, -1000000000.0).astype(F32)
 
+    rows = got.shape[0]
+    theirs[pl.ds(pl.multiple_of((band % 2) * rows, 16), rows)] = got[...]
+    theirs[pl.ds(pl.multiple_of((1 - band % 2) * rows, 16), rows)] = passed[...]
+    w_parts = (mine, theirs)
     n_a = 3 * e_loc * 3 // 2
-    r0 = e_loc * 3 // 2
+    n_b = n_a + heads_loc * wtok
+    r0 = n_b + e_loc * 3 // 2
     r1 = r0 + ff_loc * 3 // 2
     for p in range(parts):
-        qkv = from_dense(a_parts[p][:n_a])
+        qkv = from_dense(w_parts[p][:n_a])
         rows = slice(p * e_loc, (p + 1) * e_loc)
         wq[rows] = qkv[:e_loc]
         wk[rows] = qkv[e_loc : 2 * e_loc]
         wv[rows] = qkv[2 * e_loc :]
-        wup[p * ff_loc : (p + 1) * ff_loc] = from_dense(b_parts[p][r0:r1])
+        wup[p * ff_loc : (p + 1) * ff_loc] = from_dense(w_parts[p][r0:r1])
         for i in range(ff_loc // LANES):
             lo = p * ff_loc + i * LANES
-            wdt[:, lo : lo + LANES] = b_parts[p][r1 + i * feats : r1 + (i + 1) * feats]
-    w_out = jnp.concatenate([from_dense(b_parts[p][:r0]) for p in range(parts)], axis=0)
+            down = w_parts[p][r1 + i * feats : r1 + (i + 1) * feats].astype(F32) * 0.5
+            wdt[:, lo : lo + LANES] = down.astype(BF16)
+    w_out = jnp.concatenate([from_dense(w_parts[p][n_b:r0]) for p in range(parts)], axis=0)
     wot[...] = tn(w_out, eye(heads * head_dim)).astype(BF16)
 
-    span = half * WLON
     lat = (lax.broadcasted_iota(jnp.int32, (wtok, 1), 0) // WLON) % n_rows
     closed = (lat < half) if side == 0 else (lat >= half)
     shut = jnp.where(closed, penalty, 0.0)
@@ -262,7 +316,7 @@
             rows = []
             for lev in range(levs):
                 lo = n_a + h * wtok + lev * n_rows * WLON + q_row * WLON
-                rows.append(a_parts[p][lo : lo + span].astype(F32))
+                rows.append(w_parts[p][lo : lo + span].astype(F32))
             at = (p * heads_loc + h) * LANES
             bias[:, at : at + LANES] = (
                 jnp.concatenate(rows * (LANES // qtok), axis=0).T * LOG2E + shut
@@ -276,14 +330,17 @@
     def zeros(rows):
         return jnp.zeros((rows, LANES), BF16)
 
+    s1 = {}
+
     def attention(g):
-        x = n_ref[g * GROUP : (g + 1) * GROUP]
-        x_all = x.reshape(GROUP * wtok, feats)
-        lo = q_row * WLON
-        x_q = x.reshape(GROUP * levs, n_rows * WLON, feats)[:, lo : lo + span, :]
+        x_q = n_own[g * GROUP : (g + 1) * GROUP]
+        x_h = n_halo[g * GROUP : (g + 1) * GROUP]
+        order = [x_h, x_q] if side == 0 else [x_q, x_h]
+        x_all = jnp.concatenate(order, axis=2).reshape(GROUP * wtok, feats)
+        q_all = (nt(wq[...], x_q.reshape(GROUP * qtok, feats)) * q_scale).astype(BF16)
         k_all = nt(x_all, wk[...])
         v_all = nt(wv[...], x_all).astype(BF16)
-        q_all = (nt(wq[...], x_q.reshape(GROUP * qtok, feats)) * q_scale).astype(BF16)
+        yield
         mixed = []
         for pair in range(GROUP // 2):
             k0 = k_all[2 * pair * wtok : (2 * pair + 1) * wtok]
@@ -292,13 +349,10 @@
             qa = jnp.where(first, q_t, zero)
             qb = jnp.where(first, zero, q_t)
             v_t = v_all[:, 2 * pair * wtok : (2 * pair + 2) * wtok]
-            probs, inverse = [], []
+            out = []
             for e0 in range(0, e_all, LANES):
                 dims = min(LANES, e_all - e0)
-                if dims == LANES:
-                    lhs = jnp.concatenate([k0[:, e0 : e0 + LANES], k1[:, e0 : e0 + LANES]], axis=1)
-                else:
-                    lhs = jnp.concatenate([k0[:, e0 : e0 + dims], k1[:, e0 : e0 + dims]], axis=1)
+                lhs = jnp.concatenate([k0[:, e0 : e0 + dims], k1[:, e0 : e0 + dims]], axis=1)
                 columns = []
                 for h in range(dims // head_dim):
                     a = e0 + h * head_dim
@@ -312,46 +366,65 @@
                             col.append(zeros(gaps[1]))
                     columns.append(jnp.concatenate(col, axis=0))
                 s = nn(lhs.astype(BF16), jnp.concatenate(columns, axis=1))
-                for h in range(dims // head_dim):
-                    at = (e0 // head_dim + h) * LANES
-                    t = s[:, h * LANES : (h + 1) * LANES] + bias[:, at : at + LANES]
-                    p = jnp.exp2(t - jnp.max(t, axis=0, keepdims=True))
-                    inverse.append(1.0 / jnp.sum(p, axis=0, keepdims=True))
-                    p = p.astype(BF16)
-                    probs.append(
-                        jnp.concatenate([jnp.where(first, p, zero), jnp.where(first, zero, p)], axis=0)
-                    )
-            out = []
-            for h in range(0, heads, 2):
-                o = nn(
-                    v_t[h * head_dim : (h + 2) * head_dim],
-                    jnp.concatenate(probs[h : h + 2], axis=1),
-                )
-                out.append(o[:head_dim, :LANES] * inverse[h])
-                out.append(o[head_dim:, LANES:] * inverse[h + 1])
-            mixed.append(jnp.concatenate(out, axis=0))
-        mix = jnp.concatenate(mixed, axis=1).astype(BF16)
+                yield
+                for h in range(0, dims // head_dim, 2):
+                    probs, inverse = [], []
+                    for n in (h, h + 1):
+                        at = (e0 // head_dim + n) * LANES
+                        t = s[:, n * LANES : (n + 1) * LANES] + bias[:, at : at + LANES]
+                        p = jnp.exp2(t - jnp.max(t, axis=0, keepdims=True))
+                        inverse.append(1.0 / jnp.sum(p, axis=0, keepdims=True))
+                        p = p.astype(BF16)
+                        probs.append(
+                            jnp.concatenate(
+                                [jnp.where(first, p, zero), jnp.where(first, zero, p)], axis=0
+                            )
+                        )
+                    a = e0 + h * head_dim
+                    o = nn(v_t[a : a + 2 * head_dim], jnp.concatenate(probs, axis=1))
+                    out.append(o[:head_dim, :LANES] * inverse[0])
+                    out.append(o[head_dim:, LANES:] * inverse[1])
+                    yield
+            mixed.append(jnp.concatenate(out, axis=0).astype(BF16))
         at = g * GROUP * qtok
-        return nn(wot[...], mix) + raw[:, at : at + GROUP * qtok].astype(F32)
-
-    def feed_forward(g, s1):
-        c = s1 - jnp.mean(s1, axis=0, keepdims=True)
+        mix = jnp.concatenate(mixed, axis=1)
+        s1[g] = nn(wot[...], mix) + raw[:, at : at + GROUP * qtok].astype(F32)
+        yield
+
+    def feed_forward(g):
+        x = s1.pop(g)
+        c = x - jnp.mean(x, axis=0, keepdims=True)
         v = jnp.mean(c * c, axis=0, keepdims=True)
         n2 = (c * lax.rsqrt(v + 1e-05)).astype(BF16)
-        total = s1
+        yield
+        total = x
         step = 2 * LANES
         for i in range(0, ff_loc * parts, step):
-            act = gelu(nn(wup[i : i + step], n2)).astype(BF16)
+            up = nn(wup[i : i + step], n2)
+            yield
+            act = (up + up * lax.erf(up * math.sqrt(0.5))).astype(BF16)
             total = total + nn(wdt[:, i : i + step], act)
+            yield
         f = tn(total.astype(BF16), hw[...])
+        yield
         for w in range(GROUP):
             at = (g * GROUP + w) * WLON
             fscr[:, :, at : at + WLON, :] = f[w * qtok : (w + 1) * qtok].reshape(
                 levs, half, WLON, width
             )
-
-    for g in range(windows // GROUP):
-        feed_forward(g, attention(g))
+        yield
+
+    groups = windows // GROUP
+    for g in range(groups + 1):
+        tasks = []
+        if g:
+            tasks.append(feed_forward(g - 1))
+        if g < groups:
+            tasks.append(attention(g))
+        while tasks:
+            for task in list(tasks):
+                if next(task, tasks) is tasks:
+                    tasks.remove(task)
 
     patches = half * (cols // dests)
     for lev in range(levs):
@@ -361,15 +434,17 @@
             outs[d][lev] = o[:, d * patches : (d + 1) * patches]
 
 
-def forecast(n_win, raw, hw, perm, a_parts, b_parts, *, side, dests, levs, n_rows, heads_loc):
-    windows, wtok, feats = n_win.shape
+def forecast(n_halo, n_own, raw, hw, perm, weights, *, side, dests, heads_loc):
+    windows, levs, span, feats = n_own.shape
     cols = windows * WLON
-    half = n_rows // 2
-    parts = len(a_parts)
+    half = span // WLON
+    parts = 2
     head_dim = feats // (heads_loc * parts)
     e_loc = heads_loc * head_dim
     width = hw.shape[1]
-    ff_loc = (b_parts[0].shape[0] - e_loc * 3 // 2) * 2 * LANES // (3 * LANES + 2 * feats)
+    wtok = 2 * levs * span
+    rows = weights[0].shape[0] - 4 * (e_loc * 3 // 2) - heads_loc * wtok
+    ff_loc = rows * 2 * LANES // (3 * LANES + 2 * feats)
     heads = heads_loc * parts
     patches = half * (cols // dests)
     vm = pl.BlockSpec(memory_space=pltpu.VMEM)
@@ -377,16 +452,13 @@
         functools.partial(
             forecast_kernel,
             side=side,
-            parts=parts,
             dests=dests,
             e_loc=e_loc,
             heads_loc=heads_loc,
             ff_loc=ff_loc,
-            levs=levs,
-            n_rows=n_rows,
         ),
         out_shape=[VMEM((levs, width, patches), BF16)] * dests,
-        in_specs=[vm] * (4 + 2 * parts),
+        in_specs=[vm] * 8,
         out_specs=[vm] * dests,
         scratch_shapes=[
             pltpu.VMEM((feats, feats), BF16),
@@ -397,9 +469,10 @@
             pltpu.VMEM((feats, ff_loc * parts), BF16),
             pltpu.VMEM((wtok, heads * LANES), F32),
             pltpu.VMEM((levs, half, cols, width), F32),
+            pltpu.VMEM(weights[0].shape, BF16),
         ],
         compiler_params=PARAMS,
-    )(*map(near, (n_win, raw, hw, perm, *a_parts, *b_parts)))
+    )(*map(near, (n_halo, n_own, raw, hw, perm, *weights)))
 
 
 def analysis_kernel(*refs, members, side):
@@ -513,14 +586,6 @@
     )(*args)
 
 
-def from_others(array, axis):
-    size = lax.axis_size(axis)
-    return [array] + [
-        lax.ppermute(array, axis, [(i, (i + s) % size) for i in range(size)])
-        for s in range(1, size)
-    ]
-
-
 def shards(
     prior_grids,
     w_qkv,
@@ -543,40 +608,40 @@
     heads_loc = pos_bias.shape[0]
 
     prior_t = member_grid.swapaxes(2, 3)
-    half = n_rows // 2
-    mine = lax.dynamic_slice_in_dim(prior_t, lax.axis_index("tensor") * levs, levs, 0)
+    sides = lax.axis_size("tensor")
+    mine, piece, own, top, bottom = pack(
+        prior_t, w_qkv.transpose(1, 0, 2), w_out, w_up, w_down.T, pos_bias, levs
+    )
+    got = lax.ppermute(piece, "tensor", [(i, (i + 1) % sides) for i in range(sides)])
     up = [(i, i + 1) for i in range(bands - 1)]
-    above = lax.ppermute(mine[:, half:], "band", up)
-    below = lax.ppermute(mine[:, :half], "band", [(b, a) for a, b in up])
-    a_mine, b_mine = pack(w_qkv.transpose(1, 0, 2), w_out, w_up, w_down.T, pos_bias)
-    a_parts = from_others(a_mine, "tensor")
-    b_parts = from_others(b_mine, "tensor")
+    above = lax.ppermute(bottom, "band", up)
+    below = lax.ppermute(top, "band", [(b, a) for a, b in up])
+    passed = lax.ppermute(got, "band", [(i, i ^ 1) for i in range(bands)])
     obs = (
         obs_index[0].swapaxes(1, 2),
         obs_count[0],
         obs_value[0].swapaxes(1, 2),
         obs_weight[0].swapaxes(1, 2),
     )
-    n_0, n_1, raw_0, raw_1, hw, perm, idx, value, weight = prologue(
-        zonal_offsets, prior_t, above, below, head_weight.T, obs, levs, dests
+    n_own_0, n_own_1, raw_0, raw_1, hw, perm, idx, value, weight = prepare_own(
+        zonal_offsets, own, head_weight.T, obs, dests
     )
+    n_halo_0, n_halo_1 = prepare_halo(zonal_offsets, above, below)
     cw = obs_index.shape[2]
 
     received = []
-    for side, n_win, raw in ((0, n_0, raw_0), (1, n_1, raw_1)):
+    for side, n_halo, n_own, raw in ((0, n_halo_0, n_own_0, raw_0), (1, n_halo_1, n_own_1, raw_1)):
         if received:
-            n_win, _ = lax.optimization_barrier((n_win, received[0][0]))
+            n_own, _ = lax.optimization_barrier((n_own, received[0][0]))
         sent = forecast(
-            n_win,
+            n_halo,
+            n_own,
             raw,
             hw,
             perm,
-            a_parts,
-            b_parts,
+            (mine, got, passed),
             side=side,
             dests=dests,
-            levs=levs,
-            n_rows=n_rows,
             heads_loc=heads_loc,
         )
         pieces = [sent[0]]

time: 54.7 us -> 49.4 us (0.903)
  waiting for transfers between devices: 10.8 us -> 8.29 us
  local copies, waits for them, and re-layouts: 1.44 us -> 0.02 us
  starting transfers between devices: 15.9 us -> 14.8 us
    ppermute x4, waiting for transfers between devices: 6.79 us -> 3.71 us  [the longest x1 3.7 us: shards(): lax.ppermute(piece, 'tensor', [(i, (i + 1) % sides) for i in range(sides)])]
    dynamic_slice x1 -> x0, local copies, waits for them, and re-layouts: 1.34 us -> none  [shards(): lax.dynamic_slice_in_dim(prior_t, lax.axis_index('tensor') * levs, levs, 0)]
    ppermute x6, starting transfers between devices: 9.68 us -> 8.94 us  [shards(): lax.ppermute(sent[k], 'member', [(i, i ^ k) for i in range(dests)])]
    ppermute x6, waiting for transfers between devices: 3.98 us -> 4.58 us  [shards(): lax.ppermute(sent[k], 'member', [(i, i ^ k) for i in range(dests)])]
    pallas_call x4 -> x5, Pallas kernels: 20.2 us -> 20.2 us  [the longest x2 13.9 us: forecast(): pl.pallas_call(functools.partial(forecast_kernel, side=side, dests=dests,...]
  transfers between devices with their start and end apart: 10 -> 10, of which waited for: 3 -> 3; matrix products, arithmetic and copies ran while one was open for 0% -> 0% of each run, Pallas kernels for 27% -> 28%
where the time goes in v1:
time: 49.4 us; the launch traced here: 49.2 us
  Pallas kernels  25.3 us (51%)
  starting transfers between devices  14.8 us (30%)
  waiting for transfers between devices  8.29 us (17%)
  between operations  0.79 us (2%)
    pallas_call x2, Pallas kernels, forecast(): pl.pallas_call(functools.partial(forecast_kernel, side=side, dests=dests,...  13.9 us
    ppermute x6, starting transfers between devices, shards(): lax.ppermute(sent[k], 'member', [(i, i ^ k) for i in range(dests)])  8.94 us
    pallas_call x2, Pallas kernels, analysis(): pl.pallas_call(functools.partial(analysis_kernel, members=members, side=s...  5.13 us
    ppermute x6, waiting for transfers between devices, shards(): lax.ppermute(sent[k], 'member', [(i, i ^ k) for i in range(dests)])  4.58 us
    ppermute x1, waiting for transfers between devices, shards(): lax.ppermute(piece, 'tensor', [(i, (i + 1) % sides) for i in range(sides)])  3.7 us
    ppermute x1, starting transfers between devices, shards(): lax.ppermute(piece, 'tensor', [(i, (i + 1) % sides) for i in range(sides)])  3.05 us
    pallas_call x1, Pallas kernels, prepare_own(): pl.pallas_call(own_kernel, out_shape=(n_shape, n_shape, raw_shape, raw_sh...  2.84 us
    pallas_call x1, Pallas kernels, pack(): pl.pallas_call(pack_kernel, out_shape=(VMEM((rows, LANES), BF16), VMEM((r...  1.78 us
  transfers between devices with their start and end apart: 10, of which 3 were waited for; matrix products, arithmetic and copies ran while one was open for 0% of the time, Pallas kernels for 28%

profile of v1, /device:TPU:0, one launch (start us, length us, event | category | flops | bytes accessed | tf_op | source)
XLA Modules:
  0.0 49.2 jit_solution(2502855211146080244)
XLA Ops:
  0.0 0.0 copy-start
  0.0 0.0 copy-start.1
  0.0 0.0 copy-start.4
  0.0 0.0 copy-start.2
  0.0 0.0 copy-start.3
  0.0 1.8 %pack.1 = (bf16[2112,128]{1,0:T(8,128)(2,1)S(1)}, bf16[1056,128]{1,0:T(8,128)(2,1)S(1)}, bf16[2,8,192,128]{3,2,1,0:T(8,128)(2,1)S(1)}, bf16[2,4,192,128]{3,2,1,0:T(8,128)(2,1)S(1)}, bf16[2,4,192,128]{3,2,1,0:T(8,128)(2,1)S(1)}) custom-call(bf16[4,8,192,128]{3,2,1,0:T(8,128)(2,1)} %bitcast.21, bf16[3,192,96]{2,1,0:T(8,128)(2,1)} %bitcast.22, ...), custom_call_target="tpu_custom_call" | custom-call | tf_op jit(solution)/shard_map/pack/pallas_call | solution.py:115
  1.8 3.1 %collective-permute-start.2 = (bf16[1056,128]{1,0:T(8,128)(2,1)S(1)}, bf16[1056,128]{1,0:T(8,128)(2,1)S(1)}, u32[]{:S(2)}, u32[]{:S(2)}) collective-permute-start(bf16[1056,128]{1,0:T(8,128)(2,1)S(1)} %get-tuple-element.41), channel_id=1, source_target_pairs={{0,1},{1,0},{2,3},{3,2},{4,5},{5,4},{6,7},{7,6},{8,9},{9,8},{10,11... | collective-permute-start | bytes 811016 | tf_op jit(solution)/shard_map/ppermute | solution.py:615
  4.9 1.5 %collective-permute-start = (bf16[2,4,192,128]{3,2,1,0:T(8,128)(2,1)S(1)}, bf16[2,4,192,128]{3,2,1,0:T(8,128)(2,1)S(1)}, u32[]{:S(2)}, u32[]{:S(2)}) collective-permute-start(bf16[2,4,192,128]{3,2,1,0:T(8,128)(2,1)S(1)} %get-tuple-element.30), channel_id=1, source_target_pairs={{0,2},{2,4},{4,6},{1,3},{3,5},{5,7},{8,10},{10,12},{12,14},{9,11},... | collective-permute-start | bytes 1179656 | tf_op jit(solution)/shard_map/ppermute | solution.py:617
  6.3 1.3 %collective-permute-start.1 = (bf16[2,4,192,128]{3,2,1,0:T(8,128)(2,1)S(1)}, bf16[2,4,192,128]{3,2,1,0:T(8,128)(2,1)S(1)}, u32[]{:S(2)}, u32[]{:S(2)}) collective-permute-start(bf16[2,4,192,128]{3,2,1,0:T(8,128)(2,1)S(1)} %get-tuple-element.31), channel_id=1, source_target_pairs={{2,0},{4,2},{6,4},{3,1},{5,3},{7,5},{10,8},{12,10},{14,12},{11,9},... | collective-permute-start | bytes 1179656 | tf_op jit(solution)/shard_map/ppermute | solution.py:618
  7.6 3.7 %collective-permute-done.2.refs_6_ = bf16[1056,128]{1,0:T(8,128)(2,1)S(1)} collective-permute-done((bf16[1056,128]{1,0:T(8,128)(2,1)S(1)}, bf16[1056,128]{1,0:T(8,128)(2,1)S(1)}, u32[]{:S(2)}, u32[]{:S(2)}) %collective-permute-start.2) | collective-permute-done | bytes 270368 | tf_op jit(solution)/shard_map/ppermute | solution.py:615
  11.3 0.0 collective-permute-start.3
  12.0 0.0 copy-done
  12.0 0.0 copy-done.1
  12.0 0.0 copy-done.4
  12.0 0.0 copy-done.2
  12.0 0.0 copy-done.3
  12.0 2.8 %prepare_own.1 = (bf16[16,2,32,192]{3,2,1,0:T(8,128)(2,1)S(1)}, bf16[16,2,32,192]{3,2,1,0:T(8,128)(2,1)S(1)}, bf16[192,1024]{1,0:T(8,128)(2,1)S(1)}, bf16[192,10...) custom-call(s32[1]{0:T(128)S(6)} %copy.15.offs, ...), custom_call_target="tpu_custom_call" | custom-call | tf_op jit(solution)/shard_map/prepare_own/pallas_call | solution.py:218
  14.9 0.0 collective-permute-done.above
  14.9 0.0 collective-permute-done.1.below
  14.9 1.6 %prepare_halo.1 = (bf16[16,2,32,192]{3,2,1,0:T(8,128)(2,1)S(1)}, bf16[16,2,32,192]{3,2,1,0:T(8,128)(2,1)S(1)}) custom-call(s32[1]{0:T(128)S(6)} %copy.15.offs, bf16[2,4,192,128]{3,2,1,0:T(8,128)(2,1)S(1)} %collective-permute-done.above, bf16[2,4,192,128]{3,2,1,0:T(8,128)(2,1)S(1)} %collective-permute-done.1.below), custom_call_target="tpu_custom_call" | custom-call | tf_op jit(solution)/shard_map/prepare_halo/pallas_call | solution.py:257
  16.6 0.0 collective-permute-done.3.refs_7_
  16.6 7.0 %shard_map.118 = (bf16[2,160,128]{2,1,0:T(8,128)(2,1)S(1)}, bf16[2,160,128]{2,1,0:T(8,128)(2,1)S(1)}, bf16[2,160,128]{2,1,0:T(8,128)(2,1)S(1)}, bf16[2,160,128]{2,1,0:T(8,128)(2,1)S(1)}) custom-call(bf16[16,2,32,192]{3,2,1,0:T(8,128)(2,1)S(1)} %get-tuple-element.35.refs_0_, bf16[16,2,32,192]{3,2,1,0:T(8,128)(2,1)S(1)} %get-tuple-element.36.refs_1_, ...), custom_call_target="tpu_custom_call" | custom-call | tf_op jit(solution)/shard_map/pallas_call | solution.py:451
  23.5 1.9 %collective-permute-start.7 = (bf16[2,160,128]{2,1,0:T(8,128)(2,1)S(1)}, bf16[2,160,128]{2,1,0:T(8,128)(2,1)S(1)}, u32[]{:S(2)}, u32[]{:S(2)}) collective-permute-start(bf16[2,160,128]{2,1,0:T(8,128)(2,1)S(1)} %get-tuple-element.52), channel_id=1, source_target_pairs={{0,8},{8,0},{16,24},{24,16},{1,9},{9,1},{17,25},{25,17},{2,10},{10... | collective-permute-start | bytes 245768 | tf_op jit(solution)/shard_map/ppermute | solution.py:649
  25.4 2.6 %collective-permute-start.8 = (bf16[2,160,128]{2,1,0:T(8,128)(2,1)S(1)}, bf16[2,160,128]{2,1,0:T(8,128)(2,1)S(1)}, u32[]{:S(2)}, u32[]{:S(2)}) collective-permute-start(bf16[2,160,128]{2,1,0:T(8,128)(2,1)S(1)} %get-tuple-element.53), channel_id=1, source_target_pairs={{0,16},{8,24},{16,0},{24,8},{1,17},{9,25},{17,1},{25,9},{2,18},{10... | collective-permute-start | bytes 245768 | tf_op jit(solution)/shard_map/ppermute | solution.py:649
  28.0 0.0 collective-permute-start.9
  28.0 7.0 %shard_map.119 = (bf16[2,160,128]{2,1,0:T(8,128)(2,1)S(1)}, bf16[2,160,128]{2,1,0:T(8,128)(2,1)S(1)}, bf16[2,160,128]{2,1,0:T(8,128)(2,1)S(1)}, bf16[2,160,128]{2,1,0:T(8,128)(2,1)S(1)}) custom-call(bf16[16,2,32,192]{3,2,1,0:T(8,128)(2,1)S(1)} %get-tuple-element.32.refs_0_, bf16[16,2,32,192]{3,2,1,0:T(8,128)(2,1)S(1)} %get-tuple-element.43.refs_1_, ...), custom_call_target="tpu_custom_call" | custom-call | tf_op jit(solution)/shard_map/pallas_call | solution.py:451
  35.0 1.0 %collective-permute-start.4 = (bf16[2,160,128]{2,1,0:T(8,128)(2,1)S(1)}, bf16[2,160,128]{2,1,0:T(8,128)(2,1)S(1)}, u32[]{:S(2)}, u32[]{:S(2)}) collective-permute-start(bf16[2,160,128]{2,1,0:T(8,128)(2,1)S(1)} %get-tuple-element.46), channel_id=1, source_target_pairs={{0,8},{8,0},{16,24},{24,16},{1,9},{9,1},{17,25},{25,17},{2,10},{10... | collective-permute-start | bytes 245768 | tf_op jit(solution)/shard_map/ppermute | solution.py:649
  35.9 3.5 %collective-permute-start.5 = (bf16[2,160,128]{2,1,0:T(8,128)(2,1)S(1)}, bf16[2,160,128]{2,1,0:T(8,128)(2,1)S(1)}, u32[]{:S(2)}, u32[]{:S(2)}) collective-permute-start(bf16[2,160,128]{2,1,0:T(8,128)(2,1)S(1)} %get-tuple-element.47), channel_id=1, source_target_pairs={{0,16},{8,24},{16,0},{24,8},{1,17},{9,25},{17,1},{25,9},{2,18},{10... | collective-permute-start | bytes 245768 | tf_op jit(solution)/shard_map/ppermute | solution.py:649
  39.4 0.0 collective-permute-done.7.refs_1_
  39.4 0.0 collective-permute-start.6
  39.4 0.0 collective-permute-done.8.refs_2_
  39.5 0.0 collective-permute-done.9.refs_3_
  39.5 2.6 %shard_map.120.refs_7_ = f32[4,2,8,32,160]{4,3,2,1,0:T(8,128)} custom-call(bf16[2,160,128]{2,1,0:T(8,128)(2,1)S(1)} %get-tuple-element.42.refs_0_, bf16[2,160,128]{2,1,0:T(8,128)(2,1)S(1)} %collective-permute-done.7.refs_1_, bf16[2,160,128]{2,1,0:T(8,128)(2,1)S(1)} %collective-permute-done.8.refs_2_, ...), custom_call_target="tpu_custom_call" | custom-call | tf_op jit(solution)/shard_map/pallas_call | solution.py:578
  42.0 0.0 collective-permute-done.4.refs_1_
  42.0 1.0 %collective-permute-done.5.refs_2_ = bf16[2,160,128]{2,1,0:T(8,128)(2,1)S(1)} collective-permute-done((bf16[2,160,128]{2,1,0:T(8,128)(2,1)S(1)}, bf16[2,160,128]{2,1,0:T(8,128)(2,1)S(1)}, u32[]{:S(2)}, u32[]{:S(2)}) %collective-permute-start.5) | collective-permute-done | bytes 81952 | tf_op jit(solution)/shard_map/ppermute | solution.py:649
  43.1 3.5 %collective-permute-done.6.refs_3_ = bf16[2,160,128]{2,1,0:T(8,128)(2,1)S(1)} collective-permute-done((bf16[2,160,128]{2,1,0:T(8,128)(2,1)S(1)}, bf16[2,160,128]{2,1,0:T(8,128)(2,1)S(1)}, u32[]{:S(2)}, u32[]{:S(2)}) %collective-permute-start.6) | collective-permute-done | bytes 81952 | tf_op jit(solution)/shard_map/ppermute | solution.py:649
  46.6 2.6 %shard_map.121 = f32[4,2,8,32,160]{4,3,2,1,0:T(8,128)} custom-call(bf16[2,160,128]{2,1,0:T(8,128)(2,1)S(1)} %get-tuple-element.45.refs_0_, bf16[2,160,128]{2,1,0:T(8,128)(2,1)S(1)} %collective-permute-done.4.refs_1_, bf16[2,160,128]{2,1,0:T(8,128)(2,1)S(1)} %collective-permute-done.5.refs_2_, ...), custom_call_target="tpu_custom_call", output_to_operand_aliasing={{}: (7, {})} | custom-call | tf_op jit(solution)/shard_map/pallas_call | solution.py:578
Async XLA Ops:
  0.0 12.0 %copy-start = (bf16[192,160]{0,1:T(8,128)(2,1)S(1)}, bf16[192,160]{0,1:T(8,128)(2,1)}, u32[]{:S(2)}) copy-start(bf16[192,160]{0,1:T(8,128)(2,1)} %param.17) | copy-start | bytes 184324
  0.0 12.0 %copy-start.1 = (s32[1,8,32,16]{2,3,1,0:T(8,128)S(1)}, s32[1,8,32,16]{2,3,1,0:T(8,128)}, u32[]{:S(2)}) copy-start(s32[1,8,32,16]{2,3,1,0:T(8,128)} %param.20) | copy-start | bytes 49156
  0.0 12.0 %copy-start.4 = (s32[1,8,32]{2,1,0:T(8,128)S(1)}, s32[1,8,32]{2,1,0:T(8,128)}, u32[]{:S(2)}) copy-start(s32[1,8,32]{2,1,0:T(8,128)} %param.21) | copy-start | bytes 3076
  0.0 12.0 %copy-start.2 = (f32[1,8,32,16]{2,3,1,0:T(8,128)S(1)}, f32[1,8,32,16]{2,3,1,0:T(8,128)}, u32[]{:S(2)}) copy-start(f32[1,8,32,16]{2,3,1,0:T(8,128)} %param.22) | copy-start | bytes 49156
  0.0 12.0 %copy-start.3 = (f32[1,8,32,16]{2,3,1,0:T(8,128)S(1)}, f32[1,8,32,16]{2,3,1,0:T(8,128)}, u32[]{:S(2)}) copy-start(f32[1,8,32,16]{2,3,1,0:T(8,128)} %param.23) | copy-start | bytes 49156
  1.8 9.5 %collective-permute-start.2 = (bf16[1056,128]{1,0:T(8,128)(2,1)S(1)}, bf16[1056,128]{1,0:T(8,128)(2,1)S(1)}, u32[]{:S(2)}, u32[]{:S(2)}) collective-permute-start(bf16[1056,128]{1,0:T(8,128)(2,1)S(1)} %get-tuple-element.41), channel_id=1, source_target_pairs={{0,1},{1,0},{2,3},{3,2},{4,5},{5,4},{6,7},{7,6},{8,9},{9,8},{10,11... | collective-permute-start | bytes 811016 | tf_op jit(solution)/shard_map/ppermute | solution.py:615
  4.9 10.0 %collective-permute-start = (bf16[2,4,192,128]{3,2,1,0:T(8,128)(2,1)S(1)}, bf16[2,4,192,128]{3,2,1,0:T(8,128)(2,1)S(1)}, u32[]{:S(2)}, u32[]{:S(2)}) collective-permute-start(bf16[2,4,192,128]{3,2,1,0:T(8,128)(2,1)S(1)} %get-tuple-element.30), channel_id=1, source_target_pairs={{0,2},{2,4},{4,6},{1,3},{3,5},{5,7},{8,10},{10,12},{12,14},{9,11},... | collective-permute-start | bytes 1179656 | tf_op jit(solution)/shard_map/ppermute | solution.py:617
  6.3 8.6 %collective-permute-start.1 = (bf16[2,4,192,128]{3,2,1,0:T(8,128)(2,1)S(1)}, bf16[2,4,192,128]{3,2,1,0:T(8,128)(2,1)S(1)}, u32[]{:S(2)}, u32[]{:S(2)}) collective-permute-start(bf16[2,4,192,128]{3,2,1,0:T(8,128)(2,1)S(1)} %get-tuple-element.31), channel_id=1, source_target_pairs={{2,0},{4,2},{6,4},{3,1},{5,3},{7,5},{10,8},{12,10},{14,12},{11,9},... | collective-permute-start | bytes 1179656 | tf_op jit(solution)/shard_map/ppermute | solution.py:618
  11.3 5.2 %collective-permute-start.3 = (bf16[1056,128]{1,0:T(8,128)(2,1)S(1)}, bf16[1056,128]{1,0:T(8,128)(2,1)S(1)}, u32[]{:S(2)}, u32[]{:S(2)}) collective-permute-start(bf16[1056,128]{1,0:T(8,128)(2,1)S(1)} %collective-permute-done.2.refs_6_), channel_id=1, source_target_pairs={{0,2},{2,0},{4,6},{6,4},{1,3},{3,1},{5,7},{7,5},{8,10},{10,8},{12,... | collective-permute-start | bytes 811016 | tf_op jit(solution)/shard_map/ppermute | solution.py:619
  23.5 15.9 %collective-permute-start.7 = (bf16[2,160,128]{2,1,0:T(8,128)(2,1)S(1)}, bf16[2,160,128]{2,1,0:T(8,128)(2,1)S(1)}, u32[]{:S(2)}, u32[]{:S(2)}) collective-permute-start(bf16[2,160,128]{2,1,0:T(8,128)(2,1)S(1)} %get-tuple-element.52), channel_id=1, source_target_pairs={{0,8},{8,0},{16,24},{24,16},{1,9},{9,1},{17,25},{25,17},{2,10},{10... | collective-permute-start | bytes 245768 | tf_op jit(solution)/shard_map/ppermute | solution.py:649
  25.4 14.0 %collective-permute-start.8 = (bf16[2,160,128]{2,1,0:T(8,128)(2,1)S(1)}, bf16[2,160,128]{2,1,0:T(8,128)(2,1)S(1)}, u32[]{:S(2)}, u32[]{:S(2)}) collective-permute-start(bf16[2,160,128]{2,1,0:T(8,128)(2,1)S(1)} %get-tuple-element.53), channel_id=1, source_target_pairs={{0,16},{8,24},{16,0},{24,8},{1,17},{9,25},{17,1},{25,9},{2,18},{10... | collective-permute-start | bytes 245768 | tf_op jit(solution)/shard_map/ppermute | solution.py:649
  28.0 11.4 %collective-permute-start.9 = (bf16[2,160,128]{2,1,0:T(8,128)(2,1)S(1)}, bf16[2,160,128]{2,1,0:T(8,128)(2,1)S(1)}, u32[]{:S(2)}, u32[]{:S(2)}) collective-permute-start(bf16[2,160,128]{2,1,0:T(8,128)(2,1)S(1)} %get-tuple-element.54), channel_id=1, source_target_pairs={{0,24},{8,16},{16,8},{24,0},{1,25},{9,17},{17,9},{25,1},{2,26},{10... | collective-permute-start | bytes 245768 | tf_op jit(solution)/shard_map/ppermute | solution.py:649
  35.0 7.0 %collective-permute-start.4 = (bf16[2,160,128]{2,1,0:T(8,128)(2,1)S(1)}, bf16[2,160,128]{2,1,0:T(8,128)(2,1)S(1)}, u32[]{:S(2)}, u32[]{:S(2)}) collective-permute-start(bf16[2,160,128]{2,1,0:T(8,128)(2,1)S(1)} %get-tuple-element.46), channel_id=1, source_target_pairs={{0,8},{8,0},{16,24},{24,16},{1,9},{9,1},{17,25},{25,17},{2,10},{10... | collective-permute-start | bytes 245768 | tf_op jit(solution)/shard_map/ppermute | solution.py:649
  35.9 7.1 %collective-permute-start.5 = (bf16[2,160,128]{2,1,0:T(8,128)(2,1)S(1)}, bf16[2,160,128]{2,1,0:T(8,128)(2,1)S(1)}, u32[]{:S(2)}, u32[]{:S(2)}) collective-permute-start(bf16[2,160,128]{2,1,0:T(8,128)(2,1)S(1)} %get-tuple-element.47), channel_id=1, source_target_pairs={{0,16},{8,24},{16,0},{24,8},{1,17},{9,25},{17,1},{25,9},{2,18},{10... | collective-permute-start | bytes 245768 | tf_op jit(solution)/shard_map/ppermute | solution.py:649
  39.4 7.2 %collective-permute-start.6 = (bf16[2,160,128]{2,1,0:T(8,128)(2,1)S(1)}, bf16[2,160,128]{2,1,0:T(8,128)(2,1)S(1)}, u32[]{:S(2)}, u32[]{:S(2)}) collective-permute-start(bf16[2,160,128]{2,1,0:T(8,128)(2,1)S(1)} %get-tuple-element.48), channel_id=1, source_target_pairs={{0,24},{8,16},{16,8},{24,0},{1,25},{9,17},{17,9},{25,1},{2,26},{10... | collective-permute-start | bytes 245768 | tf_op jit(solution)/shard_map/ppermute | solution.py:649

commit v2 on v1

--- a/solution.py
+++ b/solution.py
@@ -188,7 +188,7 @@
     ident = eye(feats)
     for side in range(2):
 
-        def one_level(lev, carry, side=side):
+        for lev in range(levs):
             for r in range(0, half, 2):
                 x0, x1 = own[lev, side * half + r], own[lev, side * half + r + 1]
                 n_refs[side][:, lev, r * WLON : (r + 2) * WLON, :] = by_window(
@@ -197,9 +197,6 @@
                 xscr[:, lev, r * WLON : (r + 2) * WLON, :] = by_window(
                     nt(rollm, x0), nt(rollm, x1)
                 )
-            return carry
-
-        lax.fori_loop(0, levs, one_level, 0)
         for w in range(0, windows, GROUP):
             x = xscr[w : w + GROUP].reshape(GROUP * qtok, feats)
             raw_refs[side][:, w * qtok : (w + GROUP) * qtok] = nt(ident, x).astype(BF16)
@@ -236,32 +233,38 @@
     )(offs, near(own), near(hw_t), *map(near, obs))
 
 
-def halo_kernel(offs, above, below, *n_refs):
-    levs, half, _, cols = above.shape
+def halo_kernel(offs, halo, n_ref):
+    levs, half, _, cols = halo.shape
     rollm = roll_matrix(offs[0], cols)
-    for side, halo in enumerate((above, below)):
-
-        def one_level(lev, carry, side=side, halo=halo):
-            for r in range(0, half, 2):
-                n_refs[side][:, lev, r * WLON : (r + 2) * WLON, :] = by_window(
-                    nt(rollm, norm_rows(halo[lev, r])), nt(rollm, norm_rows(halo[lev, r + 1]))
-                )
-            return carry
-
-        lax.fori_loop(0, levs, one_level, 0)
-
-
-def prepare_halo(offs, above, below):
-    levs, half, feats, cols = above.shape
+    for lev in range(levs):
+        for r in range(0, half, 2):
+            n_ref[:, lev, r * WLON : (r + 2) * WLON, :] = by_window(
+                nt(rollm, norm_rows(halo[lev, r])), nt(rollm, norm_rows(halo[lev, r + 1]))
+            )
+
+
+def prepare_halo(offs, halo):
+    levs, half, feats, cols = halo.shape
     vm = pl.BlockSpec(memory_space=pltpu.VMEM)
     return pl.pallas_call(
         halo_kernel,
-        out_shape=[VMEM((cols // WLON, levs, half * WLON, feats), BF16)] * 2,
-        in_specs=[pl.BlockSpec(memory_space=pltpu.SMEM), vm, vm],
-        out_specs=[vm] * 2,
+        out_shape=VMEM((cols // WLON, levs, half * WLON, feats), BF16),
+        in_specs=[pl.BlockSpec(memory_space=pltpu.SMEM), vm],
+        out_specs=vm,
         compiler_params=PARAMS,
-        name="prepare_halo",
-    )(offs, near(above), near(below))
+    )(offs, near(halo))
+
+
+def interleave(tasks):
+    kinds = [next(task) for task in tasks]
+    last = None
+    while tasks:
+        n = next((i for i, kind in enumerate(kinds) if kind != last), 0)
+        task, last = tasks.pop(n), kinds.pop(n)
+        kind = next(task, None)
+        if kind is not None:
+            tasks.append(task)
+            kinds.append(kind)
 
 
 def forecast_kernel(*refs, side, dests, e_loc, heads_loc, ff_loc):
@@ -300,13 +303,19 @@
         wq[rows] = qkv[:e_loc]
         wk[rows] = qkv[e_loc : 2 * e_loc]
         wv[rows] = qkv[2 * e_loc :]
-        wup[p * ff_loc : (p + 1) * ff_loc] = from_dense(w_parts[p][r0:r1])
-        for i in range(ff_loc // LANES):
-            lo = p * ff_loc + i * LANES
-            down = w_parts[p][r1 + i * feats : r1 + (i + 1) * feats].astype(F32) * 0.5
-            wdt[:, lo : lo + LANES] = down.astype(BF16)
-    w_out = jnp.concatenate([from_dense(w_parts[p][n_b:r0]) for p in range(parts)], axis=0)
-    wot[...] = tn(w_out, eye(heads * head_dim)).astype(BF16)
+
+    def late_weights():
+        yield "M"
+        w_out = jnp.concatenate([from_dense(w_parts[p][n_b:r0]) for p in range(parts)], axis=0)
+        wot[...] = tn(w_out, eye(heads * head_dim)).astype(BF16)
+        for p in range(parts):
+            yield "M"
+            wup[p * ff_loc : (p + 1) * ff_loc] = from_dense(w_parts[p][r0:r1])
+            for i in range(ff_loc // LANES):
+                yield "M"
+                lo = p * ff_loc + i * LANES
+                down = w_parts[p][r1 + i * feats : r1 + (i + 1) * feats].astype(F32) * 0.5
+                wdt[:, lo : lo + LANES] = down.astype(BF16)
 
     lat = (lax.broadcasted_iota(jnp.int32, (wtok, 1), 0) // WLON) % n_rows
     closed = (lat < half) if side == 0 else (lat >= half)
@@ -332,99 +341,109 @@
 
     s1 = {}
 
-    def attention(g):
+    mixed = {}
+
+    def attention(g, pair, queries):
+        yield "M"
+        at = slice(g * GROUP + 2 * pair, g * GROUP + 2 * pair + 2)
+        order = [n_halo[at], n_own[at]] if side == 0 else [n_own[at], n_halo[at]]
+        x_pair = jnp.concatenate(order, axis=2).reshape(2 * wtok, feats)
+        k_pair = nt(x_pair, wk[...])
+        k0, k1 = k_pair[:wtok], k_pair[wtok:]
+        yield "M"
+        v_t = nt(wv[...], x_pair).astype(BF16)
+        q_t = queries[:, pair * LANES : (pair + 1) * LANES]
+        qa = jnp.where(first, q_t, zero)
+        qb = jnp.where(first, zero, q_t)
+        out = []
+        for e0 in range(0, e_all, LANES):
+            dims = min(LANES, e_all - e0)
+            yield "M"
+            lhs = jnp.concatenate([k0[:, e0 : e0 + dims], k1[:, e0 : e0 + dims]], axis=1)
+            lhs = lhs.astype(BF16)
+            columns = []
+            for h in range(dims // head_dim):
+                a = e0 + h * head_dim
+                gaps = (h * head_dim, dims - (h + 1) * head_dim)
+                col = []
+                for q in (qa, qb):
+                    if gaps[0]:
+                        col.append(zeros(gaps[0]))
+                    col.append(q[a : a + head_dim])
+                    if gaps[1]:
+                        col.append(zeros(gaps[1]))
+                columns.append(jnp.concatenate(col, axis=0))
+            scores = []
+            for h in range(0, dims // head_dim, 2):
+                yield "M"
+                s = nn(lhs, jnp.concatenate(columns[h : h + 2], axis=1))
+                scores += [s[:, :LANES], s[:, LANES:]]
+            for h in range(0, dims // head_dim, 2):
+                probs, inverse = [], []
+                for n in (h, h + 1):
+                    yield "V"
+                    at = (e0 // head_dim + n) * LANES
+                    t = scores[n] + bias[:, at : at + LANES]
+                    p = jnp.exp2(t - jnp.max(t, axis=0, keepdims=True))
+                    inverse.append(1.0 / jnp.sum(p, axis=0, keepdims=True))
+                    p = p.astype(BF16)
+                    probs.append(
+                        jnp.concatenate(
+                            [jnp.where(first, p, zero), jnp.where(first, zero, p)], axis=0
+                        )
+                    )
+                yield "M"
+                a = e0 + h * head_dim
+                o = nn(v_t[a : a + 2 * head_dim], jnp.concatenate(probs, axis=1))
+                out.append(o[:head_dim, :LANES] * inverse[0])
+                out.append(o[head_dim:, LANES:] * inverse[1])
+        mixed[g, pair] = jnp.concatenate(out, axis=0).astype(BF16)
+
+    def project_queries(g):
         x_q = n_own[g * GROUP : (g + 1) * GROUP]
-        x_h = n_halo[g * GROUP : (g + 1) * GROUP]
-        order = [x_h, x_q] if side == 0 else [x_q, x_h]
-        x_all = jnp.concatenate(order, axis=2).reshape(GROUP * wtok, feats)
-        q_all = (nt(wq[...], x_q.reshape(GROUP * qtok, feats)) * q_scale).astype(BF16)
-        k_all = nt(x_all, wk[...])
-        v_all = nt(wv[...], x_all).astype(BF16)
-        yield
-        mixed = []
-        for pair in range(GROUP // 2):
-            k0 = k_all[2 * pair * wtok : (2 * pair + 1) * wtok]
-            k1 = k_all[(2 * pair + 1) * wtok : (2 * pair + 2) * wtok]
-            q_t = q_all[:, pair * LANES : (pair + 1) * LANES]
-            qa = jnp.where(first, q_t, zero)
-            qb = jnp.where(first, zero, q_t)
-            v_t = v_all[:, 2 * pair * wtok : (2 * pair + 2) * wtok]
-            out = []
-            for e0 in range(0, e_all, LANES):
-                dims = min(LANES, e_all - e0)
-                lhs = jnp.concatenate([k0[:, e0 : e0 + dims], k1[:, e0 : e0 + dims]], axis=1)
-                columns = []
-                for h in range(dims // head_dim):
-                    a = e0 + h * head_dim
-                    gaps = (h * head_dim, dims - (h + 1) * head_dim)
-                    col = []
-                    for q in (qa, qb):
-                        if gaps[0]:
-                            col.append(zeros(gaps[0]))
-                        col.append(q[a : a + head_dim])
-                        if gaps[1]:
-                            col.append(zeros(gaps[1]))
-                    columns.append(jnp.concatenate(col, axis=0))
-                s = nn(lhs.astype(BF16), jnp.concatenate(columns, axis=1))
-                yield
-                for h in range(0, dims // head_dim, 2):
-                    probs, inverse = [], []
-                    for n in (h, h + 1):
-                        at = (e0 // head_dim + n) * LANES
-                        t = s[:, n * LANES : (n + 1) * LANES] + bias[:, at : at + LANES]
-                        p = jnp.exp2(t - jnp.max(t, axis=0, keepdims=True))
-                        inverse.append(1.0 / jnp.sum(p, axis=0, keepdims=True))
-                        p = p.astype(BF16)
-                        probs.append(
-                            jnp.concatenate(
-                                [jnp.where(first, p, zero), jnp.where(first, zero, p)], axis=0
-                            )
-                        )
-                    a = e0 + h * head_dim
-                    o = nn(v_t[a : a + 2 * head_dim], jnp.concatenate(probs, axis=1))
-                    out.append(o[:head_dim, :LANES] * inverse[0])
-                    out.append(o[head_dim:, LANES:] * inverse[1])
-                    yield
-            mixed.append(jnp.concatenate(out, axis=0).astype(BF16))
+        return (nt(wq[...], x_q.reshape(GROUP * qtok, feats)) * q_scale).astype(BF16)
+
+    def project_out(g):
         at = g * GROUP * qtok
-        mix = jnp.concatenate(mixed, axis=1)
+        mix = jnp.concatenate([mixed.pop((g, p)) for p in range(GROUP // 2)], axis=1)
         s1[g] = nn(wot[...], mix) + raw[:, at : at + GROUP * qtok].astype(F32)
-        yield
 
     def feed_forward(g):
+        yield "V"
         x = s1.pop(g)
         c = x - jnp.mean(x, axis=0, keepdims=True)
         v = jnp.mean(c * c, axis=0, keepdims=True)
         n2 = (c * lax.rsqrt(v + 1e-05)).astype(BF16)
-        yield
         total = x
-        step = 2 * LANES
-        for i in range(0, ff_loc * parts, step):
-            up = nn(wup[i : i + step], n2)
-            yield
-            act = (up + up * lax.erf(up * math.sqrt(0.5))).astype(BF16)
-            total = total + nn(wdt[:, i : i + step], act)
-            yield
+        hidden = ff_loc * parts
+        acts = []
+        for i in range(0, hidden, LANES):
+            yield "M"
+            up = nn(wup[i : i + LANES], n2)
+            yield "V"
+            acts.append((up + up * lax.erf(up * math.sqrt(0.5))).astype(BF16))
+            if len(acts) == 2 or i + LANES >= hidden:
+                yield "M"
+                lo = i + LANES - LANES * len(acts)
+                total = total + nn(wdt[:, lo : i + LANES], jnp.concatenate(acts, axis=0))
+                acts = []
+        yield "M"
         f = tn(total.astype(BF16), hw[...])
-        yield
         for w in range(GROUP):
             at = (g * GROUP + w) * WLON
             fscr[:, :, at : at + WLON, :] = f[w * qtok : (w + 1) * qtok].reshape(
                 levs, half, WLON, width
             )
-        yield
 
     groups = windows // GROUP
     for g in range(groups + 1):
-        tasks = []
-        if g:
-            tasks.append(feed_forward(g - 1))
+        tasks = [feed_forward(g - 1)] if g else [late_weights()]
         if g < groups:
-            tasks.append(attention(g))
-        while tasks:
-            for task in list(tasks):
-                if next(task, tasks) is tasks:
-                    tasks.remove(task)
+            queries = project_queries(g)
+            tasks += [attention(g, p, queries) for p in range(GROUP // 2)]
+        interleave(tasks)
+        if g < groups:
+            project_out(g)
 
     patches = half * (cols // dests)
     for lev in range(levs):
@@ -613,7 +632,7 @@
         prior_t, w_qkv.transpose(1, 0, 2), w_out, w_up, w_down.T, pos_bias, levs
     )
     got = lax.ppermute(piece, "tensor", [(i, (i + 1) % sides) for i in range(sides)])
-    up = [(i, i + 1) for i in range(bands - 1)]
+    up = [(i, (i + 1) % bands) for i in range(bands)]
     above = lax.ppermute(bottom, "band", up)
     below = lax.ppermute(top, "band", [(b, a) for a, b in up])
     passed = lax.ppermute(got, "band", [(i, i ^ 1) for i in range(bands)])
@@ -626,7 +645,8 @@
     n_own_0, n_own_1, raw_0, raw_1, hw, perm, idx, value, weight = prepare_own(
         zonal_offsets, own, head_weight.T, obs, dests
     )
-    n_halo_0, n_halo_1 = prepare_halo(zonal_offsets, above, below)
+    n_halo_0 = prepare_halo(zonal_offsets, above)
+    n_halo_1 = prepare_halo(zonal_offsets, below)
     cw = obs_index.shape[2]
 
     received = []

time: 49.4 us -> 46.6 us (0.943)
  Pallas kernels: 25.3 us -> 23.3 us
  starting transfers between devices: 14.8 us -> 13.8 us
    ppermute x1, starting transfers between devices: 1.47 us -> 0.01 us  [shards(): above = lax.ppermute(bottom, 'band', up)]
    ppermute x6, waiting for transfers between devices: 4.58 us -> 3.54 us  [shards(): lax.ppermute(sent[k], 'member', [(i, i ^ k) for i in range(dests)])]
    ppermute x1, waiting for transfers between devices: 3.7 us -> 4.73 us  [shards(): lax.ppermute(piece, 'tensor', [(i, (i + 1) % sides) for i in range(sides)])]
    pallas_call x1, Pallas kernels: 2.84 us -> 2.1 us  [prepare_own(): pl.pallas_call(own_kernel, out_shape=(n_shape, n_shape, raw_shape, raw_sh...]
    pallas_call x1 -> x2, Pallas kernels: 1.64 us -> 0.99 us  [prepare_halo(): pl.pallas_call(halo_kernel, out_shape=VMEM((cols // WLON, levs, half * WL...]
    pallas_call x2, Pallas kernels: 13.9 us -> 13.3 us  [forecast(): pl.pallas_call(functools.partial(forecast_kernel, side=side, dests=dests,...]
  transfers between devices with their start and end apart: 10 -> 10, of which waited for: 3 -> 4; matrix products, arithmetic and copies ran while one was open for 0% -> 0% of each run, Pallas kernels for 28% -> 41%
where the time goes in v2:
time: 46.6 us; the launch traced here: 46.4 us
  Pallas kernels  23.3 us (50%)
  starting transfers between devices  13.8 us (30%)
  waiting for transfers between devices  8.6 us (18%)
  between operations  0.75 us (2%)
    pallas_call x2, Pallas kernels, forecast(): pl.pallas_call(functools.partial(forecast_kernel, side=side, dests=dests,...  13.3 us
    ppermute x6, starting transfers between devices, shards(): lax.ppermute(sent[k], 'member', [(i, i ^ k) for i in range(dests)])  8.97 us
    pallas_call x2, Pallas kernels, analysis(): pl.pallas_call(functools.partial(analysis_kernel, members=members, side=s...  5.12 us
    ppermute x1, waiting for transfers between devices, shards(): lax.ppermute(piece, 'tensor', [(i, (i + 1) % sides) for i in range(sides)])  4.73 us
    ppermute x6, waiting for transfers between devices, shards(): lax.ppermute(sent[k], 'member', [(i, i ^ k) for i in range(dests)])  3.54 us
    ppermute x1, starting transfers between devices, shards(): lax.ppermute(piece, 'tensor', [(i, (i + 1) % sides) for i in range(sides)])  3.05 us
    pallas_call x1, Pallas kernels, prepare_own(): pl.pallas_call(own_kernel, out_shape=(n_shape, n_shape, raw_shape, raw_sh...  2.1 us
    pallas_call x1, Pallas kernels, pack(): pl.pallas_call(pack_kernel, out_shape=(VMEM((rows, LANES), BF16), VMEM((r...  1.78 us
  transfers between devices with their start and end apart: 10, of which 4 were waited for; matrix products, arithmetic and copies ran while one was open for 0% of the time, Pallas kernels for 41%

profile of v2, /device:TPU:0, one launch (start us, length us, event | category | flops | bytes accessed | tf_op | source)
XLA Modules:
  0.0 46.4 jit_solution(9057190471210408642)
XLA Ops:
  0.0 0.0 copy-start
  0.0 0.0 copy-start.1
  0.0 0.0 copy-start.4
  0.0 0.0 copy-start.2
  0.0 0.0 copy-start.3
  0.0 1.8 %pack.1 = (bf16[2112,128]{1,0:T(8,128)(2,1)S(1)}, bf16[1056,128]{1,0:T(8,128)(2,1)S(1)}, bf16[2,8,192,128]{3,2,1,0:T(8,128)(2,1)S(1)}, bf16[2,4,192,128]{3,2,1,0:T(8,128)(2,1)S(1)}, bf16[2,4,192,128]{3,2,1,0:T(8,128)(2,1)S(1)}) custom-call(bf16[4,8,192,128]{3,2,1,0:T(8,128)(2,1)} %bitcast.21, bf16[3,192,96]{2,1,0:T(8,128)(2,1)} %bitcast.22, ...), custom_call_target="tpu_custom_call" | custom-call | tf_op jit(solution)/shard_map/pack/pallas_call | solution.py:115
  1.8 3.1 %collective-permute-start.2 = (bf16[1056,128]{1,0:T(8,128)(2,1)S(1)}, bf16[1056,128]{1,0:T(8,128)(2,1)S(1)}, u32[]{:S(2)}, u32[]{:S(2)}) collective-permute-start(bf16[1056,128]{1,0:T(8,128)(2,1)S(1)} %get-tuple-element.37), channel_id=1, source_target_pairs={{0,1},{1,0},{2,3},{3,2},{4,5},{5,4},{6,7},{7,6},{8,9},{9,8},{10,11... | collective-permute-start | bytes 811016 | tf_op jit(solution)/shard_map/ppermute | solution.py:634
  4.9 0.0 collective-permute-start.1
  4.9 1.7 %collective-permute-start = (bf16[2,4,192,128]{3,2,1,0:T(8,128)(2,1)S(1)}, bf16[2,4,192,128]{3,2,1,0:T(8,128)(2,1)S(1)}, u32[]{:S(2)}, u32[]{:S(2)}) collective-permute-start(bf16[2,4,192,128]{3,2,1,0:T(8,128)(2,1)S(1)} %get-tuple-element.28), channel_id=1, source_target_pairs={{2,0},{4,2},{6,4},{0,6},{3,1},{5,3},{7,5},{1,7},{10,8},{12,10},{14... | collective-permute-start | bytes 1179656 | tf_op jit(solution)/shard_map/ppermute | solution.py:637
  6.6 4.7 %collective-permute-done.2.refs_6_ = bf16[1056,128]{1,0:T(8,128)(2,1)S(1)} collective-permute-done((bf16[1056,128]{1,0:T(8,128)(2,1)S(1)}, bf16[1056,128]{1,0:T(8,128)(2,1)S(1)}, u32[]{:S(2)}, u32[]{:S(2)}) %collective-permute-start.2) | collective-permute-done | bytes 270368 | tf_op jit(solution)/shard_map/ppermute | solution.py:634
  11.3 0.0 collective-permute-start.3
  12.0 0.0 copy-done
  12.0 0.0 copy-done.1
  12.0 0.0 copy-done.4
  12.0 0.0 copy-done.2
  12.0 0.0 copy-done.3
  12.0 2.1 %prepare_own.1 = (bf16[16,2,32,192]{3,2,1,0:T(8,128)(2,1)S(1)}, bf16[16,2,32,192]{3,2,1,0:T(8,128)(2,1)S(1)}, bf16[192,1024]{1,0:T(8,128)(2,1)S(1)}, bf16[192,10...) custom-call(s32[1]{0:T(128)S(6)} %copy.15.offs, ...), custom_call_target="tpu_custom_call" | custom-call | tf_op jit(solution)/shard_map/prepare_own/pallas_call | solution.py:215
  14.1 0.3 collective-permute-done.1.halo
  14.5 0.5 %shard_map.119.refs_0_ = bf16[16,2,32,192]{3,2,1,0:T(8,128)(2,1)S(1)} custom-call(s32[1]{0:T(128)S(6)} %copy.15.offs, bf16[2,4,192,128]{3,2,1,0:T(8,128)(2,1)S(1)} %collective-permute-done.1.halo), custom_call_target="tpu_custom_call" | custom-call | tf_op jit(solution)/shard_map/pallas_call | solution.py:249
  15.0 0.0 collective-permute-done.3.refs_7_
  15.0 6.6 %shard_map.120 = (bf16[2,160,128]{2,1,0:T(8,128)(2,1)S(1)}, bf16[2,160,128]{2,1,0:T(8,128)(2,1)S(1)}, bf16[2,160,128]{2,1,0:T(8,128)(2,1)S(1)}, bf16[2,160,128]{2,1,0:T(8,128)(2,1)S(1)}) custom-call(bf16[16,2,32,192]{3,2,1,0:T(8,128)(2,1)S(1)} %shard_map.119.refs_0_, bf16[16,2,32,192]{3,2,1,0:T(8,128)(2,1)S(1)} %get-tuple-element.32.refs_1_, ...), custom_call_target="tpu_custom_call" | custom-call | tf_op jit(solution)/shard_map/pallas_call | solution.py:470
  21.6 1.6 %collective-permute-start.7 = (bf16[2,160,128]{2,1,0:T(8,128)(2,1)S(1)}, bf16[2,160,128]{2,1,0:T(8,128)(2,1)S(1)}, u32[]{:S(2)}, u32[]{:S(2)}) collective-permute-start(bf16[2,160,128]{2,1,0:T(8,128)(2,1)S(1)} %get-tuple-element.48), channel_id=1, source_target_pairs={{0,8},{8,0},{16,24},{24,16},{1,9},{9,1},{17,25},{25,17},{2,10},{10... | collective-permute-start | bytes 245768 | tf_op jit(solution)/shard_map/ppermute | solution.py:669
  23.2 0.0 collective-permute-done.halo
  23.2 0.5 %shard_map.118.refs_0_ = bf16[16,2,32,192]{3,2,1,0:T(8,128)(2,1)S(1)} custom-call(s32[1]{0:T(128)S(6)} %copy.15.offs, bf16[2,4,192,128]{3,2,1,0:T(8,128)(2,1)S(1)} %collective-permute-done.halo), custom_call_target="tpu_custom_call" | custom-call | tf_op jit(solution)/shard_map/pallas_call | solution.py:249
  23.7 2.6 %collective-permute-start.8 = (bf16[2,160,128]{2,1,0:T(8,128)(2,1)S(1)}, bf16[2,160,128]{2,1,0:T(8,128)(2,1)S(1)}, u32[]{:S(2)}, u32[]{:S(2)}) collective-permute-start(bf16[2,160,128]{2,1,0:T(8,128)(2,1)S(1)} %get-tuple-element.49), channel_id=1, source_target_pairs={{0,16},{8,24},{16,0},{24,8},{1,17},{9,25},{17,1},{25,9},{2,18},{10... | collective-permute-start | bytes 245768 | tf_op jit(solution)/shard_map/ppermute | solution.py:669
  26.3 0.2 collective-permute-start.9
  26.6 6.7 %shard_map.121 = (bf16[2,160,128]{2,1,0:T(8,128)(2,1)S(1)}, bf16[2,160,128]{2,1,0:T(8,128)(2,1)S(1)}, bf16[2,160,128]{2,1,0:T(8,128)(2,1)S(1)}, bf16[2,160,128]{2,1,0:T(8,128)(2,1)S(1)}) custom-call(bf16[16,2,32,192]{3,2,1,0:T(8,128)(2,1)S(1)} %shard_map.118.refs_0_, bf16[16,2,32,192]{3,2,1,0:T(8,128)(2,1)S(1)} %get-tuple-element.39.refs_1_, ...), custom_call_target="tpu_custom_call" | custom-call | tf_op jit(solution)/shard_map/pallas_call | solution.py:470
  33.3 0.8 %collective-permute-start.4 = (bf16[2,160,128]{2,1,0:T(8,128)(2,1)S(1)}, bf16[2,160,128]{2,1,0:T(8,128)(2,1)S(1)}, u32[]{:S(2)}, u32[]{:S(2)}) collective-permute-start(bf16[2,160,128]{2,1,0:T(8,128)(2,1)S(1)} %get-tuple-element.42), channel_id=1, source_target_pairs={{0,8},{8,0},{16,24},{24,16},{1,9},{9,1},{17,25},{25,17},{2,10},{10... | collective-permute-start | bytes 245768 | tf_op jit(solution)/shard_map/ppermute | solution.py:669
  34.1 3.5 %collective-permute-start.5 = (bf16[2,160,128]{2,1,0:T(8,128)(2,1)S(1)}, bf16[2,160,128]{2,1,0:T(8,128)(2,1)S(1)}, u32[]{:S(2)}, u32[]{:S(2)}) collective-permute-start(bf16[2,160,128]{2,1,0:T(8,128)(2,1)S(1)} %get-tuple-element.43), channel_id=1, source_target_pairs={{0,16},{8,24},{16,0},{24,8},{1,17},{9,25},{17,1},{25,9},{2,18},{10... | collective-permute-start | bytes 245768 | tf_op jit(solution)/shard_map/ppermute | solution.py:669
  37.5 0.0 collective-permute-done.7.refs_1_
  37.5 0.2 collective-permute-start.6
  37.8 0.0 collective-permute-done.8.refs_2_
  37.8 0.0 collective-permute-done.9.refs_3_
  37.8 2.6 %shard_map.122.refs_7_ = f32[4,2,8,32,160]{4,3,2,1,0:T(8,128)} custom-call(bf16[2,160,128]{2,1,0:T(8,128)(2,1)S(1)} %get-tuple-element.38.refs_0_, bf16[2,160,128]{2,1,0:T(8,128)(2,1)S(1)} %collective-permute-done.7.refs_1_, bf16[2,160,128]{2,1,0:T(8,128)(2,1)S(1)} %collective-permute-done.8.refs_2_, ...), custom_call_target="tpu_custom_call" | custom-call | tf_op jit(solution)/shard_map/pallas_call | solution.py:597
  40.3 0.0 collective-permute-done.4.refs_1_
  40.3 2.6 %collective-permute-done.5.refs_2_ = bf16[2,160,128]{2,1,0:T(8,128)(2,1)S(1)} collective-permute-done((bf16[2,160,128]{2,1,0:T(8,128)(2,1)S(1)}, bf16[2,160,128]{2,1,0:T(8,128)(2,1)S(1)}, u32[]{:S(2)}, u32[]{:S(2)}) %collective-permute-start.5) | collective-permute-done | bytes 81952 | tf_op jit(solution)/shard_map/ppermute | solution.py:669
  43.0 0.9 %collective-permute-done.6.refs_3_ = bf16[2,160,128]{2,1,0:T(8,128)(2,1)S(1)} collective-permute-done((bf16[2,160,128]{2,1,0:T(8,128)(2,1)S(1)}, bf16[2,160,128]{2,1,0:T(8,128)(2,1)S(1)}, u32[]{:S(2)}, u32[]{:S(2)}) %collective-permute-start.6) | collective-permute-done | bytes 81952 | tf_op jit(solution)/shard_map/ppermute | solution.py:669
  43.9 2.6 %shard_map.123 = f32[4,2,8,32,160]{4,3,2,1,0:T(8,128)} custom-call(bf16[2,160,128]{2,1,0:T(8,128)(2,1)S(1)} %get-tuple-element.41.refs_0_, bf16[2,160,128]{2,1,0:T(8,128)(2,1)S(1)} %collective-permute-done.4.refs_1_, bf16[2,160,128]{2,1,0:T(8,128)(2,1)S(1)} %collective-permute-done.5.refs_2_, ...), custom_call_target="tpu_custom_call", output_to_operand_aliasing={{}: (7, {})} | custom-call | tf_op jit(solution)/shard_map/pallas_call | solution.py:597
Async XLA Ops:
  0.0 12.0 %copy-start = (bf16[192,160]{0,1:T(8,128)(2,1)S(1)}, bf16[192,160]{0,1:T(8,128)(2,1)}, u32[]{:S(2)}) copy-start(bf16[192,160]{0,1:T(8,128)(2,1)} %param.17) | copy-start | bytes 184324
  0.0 12.0 %copy-start.1 = (s32[1,8,32,16]{2,3,1,0:T(8,128)S(1)}, s32[1,8,32,16]{2,3,1,0:T(8,128)}, u32[]{:S(2)}) copy-start(s32[1,8,32,16]{2,3,1,0:T(8,128)} %param.20) | copy-start | bytes 49156
  0.0 12.0 %copy-start.4 = (s32[1,8,32]{2,1,0:T(8,128)S(1)}, s32[1,8,32]{2,1,0:T(8,128)}, u32[]{:S(2)}) copy-start(s32[1,8,32]{2,1,0:T(8,128)} %param.21) | copy-start | bytes 3076
  0.0 12.0 %copy-start.2 = (f32[1,8,32,16]{2,3,1,0:T(8,128)S(1)}, f32[1,8,32,16]{2,3,1,0:T(8,128)}, u32[]{:S(2)}) copy-start(f32[1,8,32,16]{2,3,1,0:T(8,128)} %param.22) | copy-start | bytes 49156
  0.0 12.0 %copy-start.3 = (f32[1,8,32,16]{2,3,1,0:T(8,128)S(1)}, f32[1,8,32,16]{2,3,1,0:T(8,128)}, u32[]{:S(2)}) copy-start(f32[1,8,32,16]{2,3,1,0:T(8,128)} %param.23) | copy-start | bytes 49156
  1.8 9.5 %collective-permute-start.2 = (bf16[1056,128]{1,0:T(8,128)(2,1)S(1)}, bf16[1056,128]{1,0:T(8,128)(2,1)S(1)}, u32[]{:S(2)}, u32[]{:S(2)}) collective-permute-start(bf16[1056,128]{1,0:T(8,128)(2,1)S(1)} %get-tuple-element.37), channel_id=1, source_target_pairs={{0,1},{1,0},{2,3},{3,2},{4,5},{5,4},{6,7},{7,6},{8,9},{9,8},{10,11... | collective-permute-start | bytes 811016 | tf_op jit(solution)/shard_map/ppermute | solution.py:634
  4.9 9.6 %collective-permute-start.1 = (bf16[2,4,192,128]{3,2,1,0:T(8,128)(2,1)S(1)}, bf16[2,4,192,128]{3,2,1,0:T(8,128)(2,1)S(1)}, u32[]{:S(2)}, u32[]{:S(2)}) collective-permute-start(bf16[2,4,192,128]{3,2,1,0:T(8,128)(2,1)S(1)} %get-tuple-element.31), channel_id=1, source_target_pairs={{0,2},{2,4},{4,6},{6,0},{1,3},{3,5},{5,7},{7,1},{8,10},{10,12},{12... | collective-permute-start | bytes 1179656 | tf_op jit(solution)/shard_map/ppermute | solution.py:636
  4.9 18.3 %collective-permute-start = (bf16[2,4,192,128]{3,2,1,0:T(8,128)(2,1)S(1)}, bf16[2,4,192,128]{3,2,1,0:T(8,128)(2,1)S(1)}, u32[]{:S(2)}, u32[]{:S(2)}) collective-permute-start(bf16[2,4,192,128]{3,2,1,0:T(8,128)(2,1)S(1)} %get-tuple-element.28), channel_id=1, source_target_pairs={{2,0},{4,2},{6,4},{0,6},{3,1},{5,3},{7,5},{1,7},{10,8},{12,10},{14... | collective-permute-start | bytes 1179656 | tf_op jit(solution)/shard_map/ppermute | solution.py:637
  11.3 3.6 %collective-permute-start.3 = (bf16[1056,128]{1,0:T(8,128)(2,1)S(1)}, bf16[1056,128]{1,0:T(8,128)(2,1)S(1)}, u32[]{:S(2)}, u32[]{:S(2)}) collective-permute-start(bf16[1056,128]{1,0:T(8,128)(2,1)S(1)} %collective-permute-done.2.refs_6_), channel_id=1, source_target_pairs={{0,2},{2,0},{4,6},{6,4},{1,3},{3,1},{5,7},{7,5},{8,10},{10,8},{12,... | collective-permute-start | bytes 811016 | tf_op jit(solution)/shard_map/ppermute | solution.py:638
  21.6 16.0 %collective-permute-start.7 = (bf16[2,160,128]{2,1,0:T(8,128)(2,1)S(1)}, bf16[2,160,128]{2,1,0:T(8,128)(2,1)S(1)}, u32[]{:S(2)}, u32[]{:S(2)}) collective-permute-start(bf16[2,160,128]{2,1,0:T(8,128)(2,1)S(1)} %get-tuple-element.48), channel_id=1, source_target_pairs={{0,8},{8,0},{16,24},{24,16},{1,9},{9,1},{17,25},{25,17},{2,10},{10... | collective-permute-start | bytes 245768 | tf_op jit(solution)/shard_map/ppermute | solution.py:669
  23.7 14.1 %collective-permute-start.8 = (bf16[2,160,128]{2,1,0:T(8,128)(2,1)S(1)}, bf16[2,160,128]{2,1,0:T(8,128)(2,1)S(1)}, u32[]{:S(2)}, u32[]{:S(2)}) collective-permute-start(bf16[2,160,128]{2,1,0:T(8,128)(2,1)S(1)} %get-tuple-element.49), channel_id=1, source_target_pairs={{0,16},{8,24},{16,0},{24,8},{1,17},{9,25},{17,1},{25,9},{2,18},{10... | collective-permute-start | bytes 245768 | tf_op jit(solution)/shard_map/ppermute | solution.py:669
  26.3 11.4 %collective-permute-start.9 = (bf16[2,160,128]{2,1,0:T(8,128)(2,1)S(1)}, bf16[2,160,128]{2,1,0:T(8,128)(2,1)S(1)}, u32[]{:S(2)}, u32[]{:S(2)}) collective-permute-start(bf16[2,160,128]{2,1,0:T(8,128)(2,1)S(1)} %get-tuple-element.50), channel_id=1, source_target_pairs={{0,24},{8,16},{16,8},{24,0},{1,25},{9,17},{17,9},{25,1},{2,26},{10... | collective-permute-start | bytes 245768 | tf_op jit(solution)/shard_map/ppermute | solution.py:669
  33.3 7.0 %collective-permute-start.4 = (bf16[2,160,128]{2,1,0:T(8,128)(2,1)S(1)}, bf16[2,160,128]{2,1,0:T(8,128)(2,1)S(1)}, u32[]{:S(2)}, u32[]{:S(2)}) collective-permute-start(bf16[2,160,128]{2,1,0:T(8,128)(2,1)S(1)} %get-tuple-element.42), channel_id=1, source_target_pairs={{0,8},{8,0},{16,24},{24,16},{1,9},{9,1},{17,25},{25,17},{2,10},{10... | collective-permute-start | bytes 245768 | tf_op jit(solution)/shard_map/ppermute | solution.py:669
  34.1 8.9 %collective-permute-start.5 = (bf16[2,160,128]{2,1,0:T(8,128)(2,1)S(1)}, bf16[2,160,128]{2,1,0:T(8,128)(2,1)S(1)}, u32[]{:S(2)}, u32[]{:S(2)}) collective-permute-start(bf16[2,160,128]{2,1,0:T(8,128)(2,1)S(1)} %get-tuple-element.43), channel_id=1, source_target_pairs={{0,16},{8,24},{16,0},{24,8},{1,17},{9,25},{17,1},{25,9},{2,18},{10... | collective-permute-start | bytes 245768 | tf_op jit(solution)/shard_map/ppermute | solution.py:669
  37.5 6.3 %collective-permute-start.6 = (bf16[2,160,128]{2,1,0:T(8,128)(2,1)S(1)}, bf16[2,160,128]{2,1,0:T(8,128)(2,1)S(1)}, u32[]{:S(2)}, u32[]{:S(2)}) collective-permute-start(bf16[2,160,128]{2,1,0:T(8,128)(2,1)S(1)} %get-tuple-element.44), channel_id=1, source_target_pairs={{0,24},{8,16},{16,8},{24,0},{1,25},{9,17},{17,9},{25,1},{2,26},{10... | collective-permute-start | bytes 245768 | tf_op jit(solution)/shard_map/ppermute | solution.py:669
